TPU v7x, 128 devices: a whole 4x4x4 slice. The times are simulated.
128 devices in a mesh: pool: 2 (over z_hi), blk: 8 (over x, core), batch: 8 (over y, z_lo).
Axes of the slice: x: 4, y: 4, z: 4 (z_hi: 2, z_lo: 2; z = z_hi * 2 + z_lo), core: 2. Of those that a mesh axis runs over, the one named last changes fastest.
Arguments:
- prompt: bfloat16 [16, 1024, 4096], P(('pool', 'batch'), 'blk'), may hold values from -40 to 40
- prompt_len: int32 [2, 8], P('pool', 'batch'), may hold values from 256 to 1024
- dec_tokens: bfloat16 [4, 64, 4096], P(None, ('pool', 'batch')), may hold values from -40 to 40
- cache_k: bfloat16 [64, 4096, 1024], P(('pool', 'batch'), None, 'blk'), may hold values from -72 to 72
- cache_v: bfloat16 [64, 4096, 1024], P(('pool', 'batch'), None, 'blk'), may hold values from -6 to 6
- cache_len: int32 [64], P(('pool', 'batch')), may hold values from 1 to 4092
- assign: int32 [2, 8], P('pool', 'batch'), may hold values from 0 to 7, each once within a row
- slot: int32 [2, 8], P('pool', 'batch'), may hold values from 0 to 3
- gain: float32 [4096], replicated, may hold values from 0.5 to 1.5
- w_qkv: bfloat16 [4096, 6144], P(None, 'blk'), may hold values from -4 to 4
- w_out: bfloat16 [4096, 4096], P('blk'), may hold values from -0.09375 to 0.09375
Outputs:
- prefill_out: bfloat16 [16, 1024, 4096], P(('pool', 'batch'), 'blk')
- dec_out: bfloat16 [4, 64, 4096], P(None, ('pool', 'batch'))
Inputs may be any that keep to these rules, and one draw needn't show every extreme that they name: For each pool p, assign[p] is a permutation of the 8 stretch indices of the other pool.
All inputs are finite; a program needn't handle non-finite values.
Results may differ from a plain program's by a relative error of at most 0.011.
Values may be sent and summed in bfloat16 or wider, within the bound.
A program may use at most 128 MiB of HBM per device.

v0:
```python
import jax
import jax.numpy as jnp
from jax import lax
from jax.sharding import PartitionSpec as P

HEAD_DIM = 128
GROUP = 4


EPSILON = 1e-05
THETA = 500000.0


def swapped(array, axis, bit):
    return lax.ppermute(array, axis, [(i, i ^ 1 << bit) for i in range(lax.axis_size(axis))])


def in_one_piece(arrays, axis, dim, along):
    widths = [a.shape[along] for a in arrays]
    both = jnp.concatenate(arrays, axis=along)
    out = lax.all_gather(both, axis, axis=dim, tiled=True)
    return tuple(jnp.split(out, [sum(widths[:k]) for k in range(1, len(widths))], axis=along))


def copy_for_each(array, axis):
    copies = jnp.broadcast_to(array, (lax.axis_size(axis), *array.shape))
    return lax.all_to_all(copies, axis, split_axis=0, concat_axis=0, tiled=True)


def of_everyone(array, axis):
    everything = copy_for_each(array, axis)
    return jnp.sum(everything.astype(jnp.float32), axis=0)


def rms_norm(values, gain):
    wide = values.astype(jnp.float32)
    factor = lax.rsqrt(jnp.mean(wide * wide, axis=-1, keepdims=True) + EPSILON)
    return (wide * factor * gain).astype(jnp.bfloat16)


def rotate(vector, places):
    half = vector.shape[-1] // 2
    freqs = THETA ** (-jnp.arange(half, dtype=jnp.float32) / half)
    angles = places.astype(jnp.float32)[..., None] * freqs
    cosine = jnp.cos(angles)
    sine = jnp.sin(angles)
    first = vector[..., :half]
    second = vector[..., half:]
    return jnp.concatenate(
        [first * cosine - second * sine, second * cosine + first * sine], axis=-1
    )


def softmax_weights(scores):
    top = jnp.max(scores, axis=-1, keepdims=True)
    expo = jnp.exp(scores - top)
    return (expo / jnp.sum(expo, axis=-1, keepdims=True)).astype(jnp.bfloat16)


def make_picker(wanted, carry, piece):
    count = piece[0].shape[0]
    match = jnp.arange(count, dtype=jnp.int32) == wanted
    keys = jnp.sum(jnp.where(match[:, None, None], piece[0].astype(jnp.float32), 0.0), axis=0)
    values = jnp.sum(jnp.where(match[:, None, None], piece[1].astype(jnp.float32), 0.0), axis=0)
    length = carry[2] + jnp.sum(jnp.where(match, piece[2], 0))
    return (keys, values, length)


def attend(
    query,
    cache_key,
    cache_value,
    lengths,
    fresh,
    new_key,
    new_value,
    new_len,
    own_key,
    own_value,
    own_mask,
):
    f32 = jnp.float32
    scale = query.shape[-1] ** (-0.5)
    old = jnp.einsum("srhgd,rchd->srhgc", query, cache_key, preferred_element_type=f32) * scale
    span = jnp.arange(cache_key.shape[1], dtype=jnp.int32)
    old_ok = (span[None, :] < lengths[:, None]) & jnp.logical_not(fresh)[:, None]
    old = jnp.where(old_ok[None, :, None, None, :], old, -jnp.inf)
    new = jnp.einsum("srhgd,chd->srhgc", query, new_key, preferred_element_type=f32) * scale
    reach = jnp.arange(new_key.shape[0], dtype=jnp.int32)
    new_ok = (reach[None, :] < new_len) & fresh[:, None]
    new = jnp.where(new_ok[None, :, None, None, :], new, -jnp.inf)
    own = jnp.einsum("srhgd,trhd->srhgt", query, own_key, preferred_element_type=f32) * scale
    own = jnp.where(own_mask[:, None, None, None, :], own, -jnp.inf)
    cached = cache_key.shape[1]
    fresh_count = new_key.shape[0]
    probs = softmax_weights(jnp.concatenate([old, new, own], axis=-1))
    mixed = jnp.einsum(
        "srhgc,rchd->srhgd", probs[..., :cached], cache_value, preferred_element_type=f32
    )
    mixed = mixed + jnp.einsum(
        "srhgc,chd->srhgd",
        probs[..., cached : cached + fresh_count],
        new_value,
        preferred_element_type=f32,
    )
    mixed = mixed + jnp.einsum(
        "srhgt,trhd->srhgd",
        probs[..., cached + fresh_count :],
        own_value,
        preferred_element_type=f32,
    )
    return mixed.astype(jnp.bfloat16)


def body(
    prompt, prompt_len, dec_tokens, cache_k, cache_v, cache_len, assign, slot, gain, w_qkv, w_out
):
    f32 = jnp.float32
    bf16 = jnp.bfloat16
    local = w_out.shape[0] // (GROUP * HEAD_DIM)
    scale = HEAD_DIM ** (-0.5)
    normed = rms_norm(prompt[0], gain)
    joined = jnp.dot(
        lax.all_gather(normed, "blk", axis=0, tiled=True), w_qkv, preferred_element_type=f32
    )
    stretch = joined.shape[0]
    joined = joined.reshape(stretch, local, GROUP + 2, HEAD_DIM)
    places = jnp.arange(stretch, dtype=jnp.int32)
    query = rotate(joined[:, :, :GROUP], places[:, None, None]).astype(bf16)
    key = rotate(joined[:, :, GROUP], places[:, None]).astype(bf16)
    value = joined[:, :, GROUP + 1].astype(bf16)
    plen = prompt_len[0, 0]
    scores = jnp.einsum("qhgd,khd->hgqk", query, key, preferred_element_type=f32) * scale
    allowed = (places[None, :] <= places[:, None]) & (places[None, :] < plen)
    scores = jnp.where(allowed, scores, -jnp.inf)
    probs = softmax_weights(scores)
    mixed = jnp.einsum("hgqk,khd->qhgd", probs, value, preferred_element_type=f32).astype(bf16)
    mixed = mixed.reshape(stretch, local * GROUP * HEAD_DIM)
    rows = mixed
    summed = lax.psum_scatter(
        jnp.dot(rows, w_out, preferred_element_type=f32).astype(jnp.bfloat16),
        "blk",
        scatter_dimension=0,
        tiled=True,
    ).astype(jnp.float32)
    prefill_out = (prompt[0].astype(f32) + summed).astype(bf16)[None]
    packet = (
        key.reshape(1, stretch, local * HEAD_DIM),
        value.reshape(1, stretch, local * HEAD_DIM),
        prompt_len.reshape(1),
    )
    empty = (
        jnp.zeros((stretch, local * HEAD_DIM), f32),
        jnp.zeros((stretch, local * HEAD_DIM), f32),
        jnp.zeros((), jnp.int32),
    )
    wanted = assign[0, 0]
    crossed = swapped((packet[0], packet[1], packet[2]), "pool", 0)
    arrived = make_picker(
        wanted,
        empty,
        (
            *in_one_piece((crossed[0], crossed[1]), "batch", 0, 1),
            lax.all_gather(crossed[2], "batch", axis=0, tiled=True),
        ),
    )
    new_key = arrived[0].astype(bf16).reshape(stretch, local, HEAD_DIM)
    new_value = arrived[1].astype(bf16).reshape(stretch, local, HEAD_DIM)
    new_len = arrived[2]
    steps = dec_tokens.shape[0]
    rows = dec_tokens.shape[1]
    cached = cache_k.shape[1]
    cache_key = cache_k.reshape(rows, cached, local, HEAD_DIM)
    cache_value = cache_v.reshape(rows, cached, local, HEAD_DIM)
    fresh = jnp.arange(rows, dtype=jnp.int32) == slot[0, 0]
    begin = jnp.where(fresh, new_len, cache_len)
    normed_steps = rms_norm(dec_tokens, gain)
    joined_all = jnp.dot(normed_steps.reshape(steps * rows, -1), w_qkv, preferred_element_type=f32)
    joined_all = joined_all.reshape(steps, rows, local, GROUP + 2, HEAD_DIM)
    where_all = begin[None, :] + jnp.arange(steps, dtype=jnp.int32)[:, None]
    all_query = rotate(joined_all[:, :, :, :GROUP], where_all[:, :, None, None]).astype(bf16)
    all_key = rotate(joined_all[:, :, :, GROUP], where_all[:, :, None]).astype(bf16)
    all_value = joined_all[:, :, :, GROUP + 1].astype(bf16)
    own_mask = jnp.arange(steps)[None, :] <= jnp.arange(steps)[:, None]
    attended = attend(
        all_query,
        cache_key,
        cache_value,
        cache_len,
        fresh,
        new_key,
        new_value,
        new_len,
        all_key,
        all_value,
        own_mask,
    )
    partial_value = jnp.dot(
        attended.reshape(steps * rows, local * GROUP * HEAD_DIM), w_out, preferred_element_type=f32
    )
    total = of_everyone(partial_value.reshape(steps, rows, -1).astype(jnp.bfloat16), "blk").astype(
        jnp.float32
    )
    dec_out = (dec_tokens.astype(f32) + total).astype(bf16)
    return (prefill_out, dec_out)


def solution(mesh):
    return jax.shard_map(
        body,
        mesh=mesh,
        in_specs=(
            P(("pool", "batch"), "blk", None),
            P("pool", "batch"),
            P(None, ("pool", "batch"), None),
            P(("pool", "batch"), None, "blk"),
            P(("pool", "batch"), None, "blk"),
            P(("pool", "batch")),
            P("pool", "batch"),
            P("pool", "batch"),
            P(),
            P(None, "blk"),
            P("blk", None),
        ),
        out_specs=(P(("pool", "batch"), "blk", None), P(None, ("pool", "batch"), None)),
        check_vma=False,
    )
```

profile of v0, /device:TPU:1, one launch (start us, length us, event | category | flops | bytes accessed | tf_op | source)
XLA Modules:
  0.0 259.4 jit_solution(5367796632845972385)
XLA Ops:
  7.2 1.5 fusion.12
  8.7 2.5 fusion.14
  11.4 53.3 %all-gather.3.cloned.1.call-done = bf16[1024,4096]{1,0:T(8,128)(2,1)} async-done(((bf16[128,4096]{1,0:T(8,128)(2,1)}), bf16[1024,4096]{1,0:T(8,128)(2,1)}) %all-gather.3.cloned.1.call-update) | async-done | bytes 8388624 | tf_op jit(solution)/shard_map/all_gather | solution.py:124
  64.7 11.0 %fusion.90 = f32[1024,768]{0,1:T(8,128)S(1)} fusion(bf16[1024,4096]{1,0:T(8,128)(2,1)} %all-gather.3.cloned.1.call-done, bf16[4096,768]{1,0:T(8,128)(2,1)} %param.20), kind=kOutput, calls=%fused_computation.146 | convolution fusion | flops 6442450944 | bytes 17825792 | tf_op jit(solution)/shard_map/dot_general | solution.py:123
  75.7 1.6 copy-done.2
  77.6 3.0 %collective-permute-start.2 = (bf16[1,1024,128]{2,1,0:T(8,128)(2,1)S(1)}, bf16[1,1024,128]{2,1,0:T(8,128)(2,1)S(1)}, u32[]{:S(2)}, u32[]{:S(2)}) collective-permute-start(bf16[1,1024,128]{2,1,0:T(8,128)(2,1)S(1)} %bitcast.190), channel_id=1, source_target_pairs={{0,64},{64,0},{1,65},{65,1},{2,66},{66,2},{3,67},{67,3},{4,68},{68... | collective-permute-start | bytes 786440 | tf_op jit(solution)/shard_map/ppermute | solution.py:15
  80.7 2.4 fusion.42
  83.5 3.3 %collective-permute-done.2 = bf16[1,1024,128]{2,1,0:T(8,128)(2,1)S(1)} collective-permute-done((bf16[1,1024,128]{2,1,0:T(8,128)(2,1)S(1)}, bf16[1,1024,128]{2,1,0:T(8,128)(2,1)S(1)}, u32[]{:S(2)}, u32[]{:S(2)}) %collective-permute-start.2) | collective-permute-done | bytes 262176 | tf_op jit(solution)/shard_map/ppermute | solution.py:15
  86.8 5.5 %collective-permute-done.1 = bf16[1,1024,128]{2,1,0:T(8,128)(2,1)S(1)} collective-permute-done((bf16[1,1024,128]{2,1,0:T(8,128)(2,1)S(1)}, bf16[1,1024,128]{2,1,0:T(8,128)(2,1)S(1)}, u32[]{:S(2)}, u32[]{:S(2)}) %collective-permute-start.1) | collective-permute-done | bytes 262176 | tf_op jit(solution)/shard_map/ppermute | solution.py:15
  94.0 3.1 %multiply_cosine_fusion = (f32[1024,64]{1,0:T(8,128)}, f32[1024,64]{1,0:T(8,128)}) fusion(f32[64]{0:T(128)S(1)} %multiply_power_fusion, f32[1024]{0:T(1024)S(1)} %iota_convert_fusion), kind=kLoop, calls=%fused_computation.56 | loop fusion | flops 65536 | bytes 528640 | tf_op jit(solution)/shard_map/cos | solution.py:45
  97.4 3.1 %fusion.86 = (f32[1024,1,4,64]{0,3,2,1:T(8,128)}, f32[1024,1,4,64]{0,3,2,1:T(8,128)}) fusion(f32[1024,1,6,128]{0,3,2,1:T(8,128)} %bitcast.185), kind=kLoop, calls=%fused_computation.142 | loop fusion | bytes 4194304 | tf_op jit(solution)/shard_map/slice | solution.py:48
  100.5 1.8 copy.131
  102.3 3.3 %copy.130 = f32[1024,1,4,64]{3,0,2,1:T(8,128)} copy(f32[1024,1,4,64]{0,3,2,1:T(8,128)} %get-tuple-element.7) | data formatting | bytes 2097152
  105.6 2.4 fusion.30
  108.1 3.8 %fusion.1 = (f32[4,1024]{1,0:T(4,128)S(1)}, f32[1024,1024,4]{1,0,2:T(8,128)S(1)}) fusion(pred[1024,1024]{0,1:T(8,128)(4,1)S(1)} %fusion.11, bf16[1024,4,64]{2,0,1:T(8,128)(2,1)S(1)} %get-tuple-element.5, bf16[1024,4,64]{2,0,1:T(8,128)(2,1)S(1)} %get-tuple-element.4, bf16[1024,64]{1,0:T(8,128)(2,1)S(1)} %bitcast.189, bf16[1024,64]{1,0:T(8,128)(2,1)S(1)} %bitcast.187), kind=kOutput, calls=%fused_computation.4 | convolution fusion | flops 1088942080 | bytes 19152896 | tf_op jit(solution)/shard_map/qhgd,khd->hgqk/dot_general | solution.py:133
  111.9 3.6 %fusion = f32[4,1024]{1,0:T(4,128)S(1)} fusion(f32[1024,1024,4]{1,0,2:T(8,128)S(1)} %get-tuple-element.19, f32[4,1024]{1,0:T(4,128)S(1)} %get-tuple-element.18, pred[1024,1024]{0,1:T(8,128)(4,1)S(1)} %fusion.11), kind=kLoop, calls=%fused_computation.3 | loop fusion | flops 16773120 | bytes 17858560 | tf_op jit(solution)/shard_map/reduce_sum | solution.py:57
  115.6 5.4 %fusion.16 = bf16[128,4,1024]{2,0,1:T(8,128)(2,1)S(1)} fusion(f32[4,1024]{1,0:T(4,128)S(1)} %fusion, f32[4,1024]{1,0:T(4,128)S(1)} %get-tuple-element.18, f32[1024,1024,4]{1,0,2:T(8,128)S(1)} %get-tuple-element.19, pred[1024,1024]{0,1:T(8,128)(4,1)S(1)} %fusion.11, bf16[1024,1,1,128]{3,0,2,1:T(8,128)(2,1)S(1)} %copy-done.7), kind=kOutput, calls=%fused_computation.31 | convolution fusion | flops 1095237632 | bytes 19169280 | tf_op jit(solution)/shard_map/hgqk,khd->qhgd/dot_general | solution.py:137
  121.0 6.8 %convolution_convert_fusion = bf16[1024,4096]{1,0:T(8,128)(2,1)} fusion(bf16[1024,512]{0,1:T(8,128)(2,1)S(1)} %bitcast.196, bf16[512,4096]{1,0:T(8,128)(2,1)S(1)} %copy-done.1), kind=kOutput, calls=%fused_computation.7 | convolution fusion | flops 4299161600 | bytes 13631488 | tf_op jit(solution)/shard_map/dot_general | solution.py:141
  127.8 3.3 %collective-permute-start = (s32[1]{0:T(128)}, s32[1]{0:T(128)}, u32[]{:S(2)}, u32[]{:S(2)}) collective-permute-start(s32[1]{0:T(128)} %bitcast.27), channel_id=1, source_target_pairs={{0,64},{64,0},{1,65},{65,1},{2,66},{66,2},{3,67},{67,3},{4,68},{68... | collective-permute-start | bytes 20 | tf_op jit(solution)/shard_map/ppermute | solution.py:15
  131.2 8.8 %copy.100 = bf16[4096,768]{0,1:T(8,128)(2,1)} copy(bf16[4096,768]{1,0:T(8,128)(2,1)} %param.20) | data formatting | bytes 12582912 | tf_op args[9]
  142.1 4.6 %convolution_bitcast_fusion = f32[4,4,1,6,128]{4,1,3,0,2:T(4,128)S(1)} fusion(bf16[6,128,4096,1]{2,1,0,3:T(8,128)(2,1)} %bitcast.181, bf16[4,4,4096]{2,1,0:T(4,128)(2,1)S(1)} %copy-done.5, f32[4096]{0:T(1024)S(1)} %copy-done.8, f32[4,4]{1,0:T(4,128)S(1)} %add_rsqrt_fusion), kind=kOutput, calls=%fused_computation.37 | convolution fusion | flops 100925440 | bytes 6488128 | tf_op jit(solution)/shard_map/dot_general | solution.py:178
  146.9 1.4 dynamic-update-slice
  148.3 10.2 %all-reduce = s32[8]{0:T(128)S(1)} all-reduce(s32[8]{0:T(128)S(1)} %dynamic-update-slice), channel_id=1, replica_groups=mesh['pool'=2,'blk'=8,'batch'=8] {'batch'}, use_global_device_ids=true, to_apply=%add | all-reduce | flops 8 | bytes 64
  161.4 3.5 %fusion.88 = (f32[4,4,4]{2,0,1:T(4,128)S(1)}, f32[4,4,1,4,4096]{4,3,0,1,2:T(4,128)S(1)}) fusion(bf16[4,4096,128]{2,1,0:T(8,128)(2,1)} %param.14, bf16[4,4,4,128]{3,1,2,0:T(4,128)(2,1)S(1)} %pad_maximum_fusion.2, pred[4,4096]{1,0:T(4,128)(4,1)S(1)} %fusion.62), kind=kOutput, calls=%fused_computation.144 | convolution fusion | flops 67895232 | bytes 5275904 | tf_op jit(solution)/shard_map/srhgd,rchd->srhgc/dot_general | solution.py:84
  164.9 18.8 %all-gather.5.cloned.1.call-done = bf16[8,2048,128]{2,1,0:T(8,128)(2,1)} async-done(((bf16[1,2048,128]{2,1,0:T(8,128)(2,1)}), bf16[8,2048,128]{2,1,0:T(8,128)(2,1)}) %all-gather.5.cloned.1.call-update) | async-done | bytes 4194320 | tf_op jit(solution)/shard_map/all_gather | solution.py:21
  183.7 3.3 %select_reduce_fusion = (bf16[1024,128]{1,0:T(8,128)(2,1)S(1)}, bf16[1024,128]{1,0:T(8,128)(2,1)S(1)}) fusion(bf16[8,2048,128]{2,1,0:T(8,128)(2,1)} %all-gather.5.cloned.1.call-done, pred[8]{0:T(512)(128)(4,1)S(1)} %iota_compare_fusion.5), kind=kLoop, calls=%fused_computation.17 | loop fusion | flops 6029312 | bytes 4718600 | tf_op jit(solution)/shard_map/reduce_sum | solution.py:64
  188.7 0.9 fusion.21
  189.8 3.0 %convolution_convert_fusion.1 = bf16[4,4,4096]{2,1,0:T(4,128)(2,1)S(1)} fusion(bf16[512,4096]{1,0:T(8,128)(2,1)} %param.21, bf16[4,4,512]{2,0,1:T(4,128)(2,1)S(1)} %dot_general.67), kind=kOutput, calls=%fused_computation.12 | convolution fusion | flops 67174400 | bytes 4341760 | tf_op jit(solution)/shard_map/dot_general | solution.py:198
  193.3 25.9 %all_to_all.5 = bf16[8,4,4,4096]{3,2,1,0:T(4,128)(2,1)S(1)} all-to-all(bf16[8,4,4,4096]{3,2,1,0:T(4,128)(2,1)S(1)} %broadcast_in_dim.124), channel_id=1, replica_groups=mesh['pool'=2,'blk'=8,'batch'=8] {'blk'}, dimensions={0} | all-to-all | bytes 2097152 | tf_op jit(solution)/shard_map/all_to_all | solution.py:27
  219.1 1.2 convert_reduce_fusion
  221.1 29.3 %reduce-scatter.2.cloned.1.call-done = bf16[128,4096]{1,0:T(8,128)(2,1)} async-done(((bf16[1024,4096]{1,0:T(8,128)(2,1)}), bf16[128,4096]{1,0:T(8,128)(2,1)}) %reduce-scatter.2.cloned.1.call-update) | async-done | bytes 1048592 | tf_op jit(solution)/shard_map/reduce_scatter | solution.py:140
  250.4 2.4 fusion.32
  (73 shorter events, 9.2 us)
Async XLA Ops:
  7.2 57.5 %all-gather.3.cloned.1.call-start = ((), (), s32[]{:S(2)}) async-start(), calls=%async_computation.2 | async-start | bytes 9437184 | tf_op jit(solution)/shard_map/all_gather | solution.py:124
  11.3 172.4 %all-gather.5.cloned.1.call-start = ((), (), s32[]{:S(2)}) async-start(), calls=%async_computation.4 | async-start | bytes 4718592 | tf_op jit(solution)/shard_map/all_gather | solution.py:21
  75.7 1.7 copy-start.2
  77.6 22.9 %copy-start.6 = (bf16[1024,1,1,128]{3,0,2,1:T(8,128)(2,1)}, bf16[1024,1,1,128]{3,0,2,1:T(8,128)(2,1)S(1)}, u32[]{:S(2)}) copy-start(bf16[1024,1,1,128]{3,0,2,1:T(8,128)(2,1)S(1)} %copy.128) | copy-start | bytes 786436
  77.6 9.2 %collective-permute-start.2 = (bf16[1,1024,128]{2,1,0:T(8,128)(2,1)S(1)}, bf16[1,1024,128]{2,1,0:T(8,128)(2,1)S(1)}, u32[]{:S(2)}, u32[]{:S(2)}) collective-permute-start(bf16[1,1024,128]{2,1,0:T(8,128)(2,1)S(1)} %bitcast.190), channel_id=1, source_target_pairs={{0,64},{64,0},{1,65},{65,1},{2,66},{66,2},{3,67},{67,3},{4,68},{68... | collective-permute-start | bytes 786440 | tf_op jit(solution)/shard_map/ppermute | solution.py:15
  83.1 17.4 %copy-start.3 = (bf16[1024,1,64]{2,0,1:T(8,128)(2,1)}, bf16[1024,1,64]{2,0,1:T(8,128)(2,1)S(1)}, u32[]{:S(2)}) copy-start(bf16[1024,1,64]{2,0,1:T(8,128)(2,1)S(1)} %get-tuple-element.9) | copy-start | bytes 393220
  83.3 8.9 %collective-permute-start.1 = (bf16[1,1024,128]{2,1,0:T(8,128)(2,1)S(1)}, bf16[1,1024,128]{2,1,0:T(8,128)(2,1)S(1)}, u32[]{:S(2)}, u32[]{:S(2)}) collective-permute-start(bf16[1,1024,128]{2,1,0:T(8,128)(2,1)S(1)} %pad_maximum_fusion.1), channel_id=1, source_target_pairs={{0,64},{64,0},{1,65},{65,1},{2,66},{66,2},{3,67},{67,3},{4,68},{68... | collective-permute-start | bytes 786440 | tf_op jit(solution)/shard_map/ppermute | solution.py:15
  93.1 157.3 %reduce-scatter.2.cloned.1.call-start = ((), (), s32[]{:S(2)}) async-start(), calls=%async_computation.3 | async-start | bytes 9437184 | tf_op jit(solution)/shard_map/reduce_scatter | solution.py:140
  105.6 2.4 copy-start.4
  111.9 3.7 %copy-start.7 = (bf16[1024,1,1,128]{3,0,2,1:T(8,128)(2,1)S(1)}, bf16[1024,1,1,128]{3,0,2,1:T(8,128)(2,1)}, u32[]{:S(2)}) copy-start(bf16[1024,1,1,128]{3,0,2,1:T(8,128)(2,1)} %copy-done.6) | copy-start | bytes 786436
  115.6 5.4 %copy-start.1 = (bf16[512,4096]{1,0:T(8,128)(2,1)S(1)}, bf16[512,4096]{1,0:T(8,128)(2,1)}, u32[]{:S(2)}) copy-start(bf16[512,4096]{1,0:T(8,128)(2,1)} %param.21) | copy-start | bytes 12582916
  127.8 19.0 %collective-permute-start = (s32[1]{0:T(128)}, s32[1]{0:T(128)}, u32[]{:S(2)}, u32[]{:S(2)}) collective-permute-start(s32[1]{0:T(128)} %bitcast.27), channel_id=1, source_target_pairs={{0,64},{64,0},{1,65},{65,1},{2,66},{66,2},{3,67},{67,3},{4,68},{68... | collective-permute-start | bytes 20 | tf_op jit(solution)/shard_map/ppermute | solution.py:15
  131.2 10.1 %copy-start.11 = (u32[128]{0:T(128)S(1)}, u32[128]{0:T(128)}, u32[]{:S(2)}) copy-start(u32[128]{0:T(128)} %constant.34) | copy-start | bytes 1540
  131.2 10.7 %copy-start.5 = (bf16[4,4,4096]{2,1,0:T(4,128)(2,1)S(1)}, bf16[4,4,4096]{2,1,0:T(4,128)(2,1)}, u32[]{:S(2)}) copy-start(bf16[4,4,4096]{2,1,0:T(4,128)(2,1)} %param.13) | copy-start | bytes 393220
  131.2 10.9 %copy-start.8 = (f32[4096]{0:T(1024)S(1)}, f32[4096]{0:T(1024)}, u32[]{:S(2)}) copy-start(f32[4096]{0:T(1024)} %param.19) | copy-start | bytes 49156
  142.1 4.7 %copy-start.9 = (s32[4]{0:T(128)S(1)}, s32[4]{0:T(128)}, u32[]{:S(2)}) copy-start(s32[4]{0:T(128)} %param.16) | copy-start | bytes 52
  183.7 5.0 %copy-start.10 = (bf16[4,4096,128]{2,1,0:T(8,128)(2,1)S(1)}, bf16[4,4096,128]{2,1,0:T(8,128)(2,1)}, u32[]{:S(2)}) copy-start(bf16[4,4096,128]{2,1,0:T(8,128)(2,1)} %param.15) | copy-start | bytes 12582916
  189.8 60.5 %copy-start = (bf16[1,128,4096]{2,1,0:T(8,128)(2,1)S(1)}, bf16[1,128,4096]{2,1,0:T(8,128)(2,1)}, u32[]{:S(2)}) copy-start(bf16[1,128,4096]{2,1,0:T(8,128)(2,1)} %param.11) | copy-start | bytes 3145732
Sparse Core Ops, SparseCore 0:
  11.4 53.2 all-gather.2
  93.2 90.4 all-gather.4
  186.1 64.2 reduce-scatter.1
where the time goes:
time: 260 us; the launch traced here: 259 us
  waiting for transfers between devices  110 us (42%)
  matrix products  39.9 us (15%)
  blocking collectives  36.1 us (14%)
  other arithmetic  28.8 us (11%)
  local copies, waits for them, and re-layouts  21.6 us (8%)
  between operations  16.1 us (6%)
  starting transfers between devices  6.76 us (3%)
    all_gather x1, waiting for transfers between devices, body(): lax.all_gather(normed, 'blk', axis=0, tiled=True)  53.3 us
    reduce_scatter x1, waiting for transfers between devices, body(): lax.psum_scatter(jnp.dot(rows, w_out, preferred_element_type=f32).astype(...  29.3 us
    all_to_all x1, blocking collectives, copy_for_each(): return lax.all_to_all(copies, axis, split_axis=0, concat_axis=0, tiled=True)  25.9 us
    all_gather x1, waiting for transfers between devices, in_one_piece(): out = lax.all_gather(both, axis, axis=dim, tiled=True)  18.8 us
    unnamed x32, local copies, waits for them, and re-layouts  18 us
    dot_general x1, matrix products, body(): jnp.dot(lax.all_gather(normed, 'blk', axis=0, tiled=True), w_qkv, preferr...  11 us
    unnamed x1, blocking collectives  10.2 us
    ppermute x3, waiting for transfers between devices, swapped(): lax.ppermute(array, axis, [(i, i ^ 1 << bit) for i in range(lax.axis_size...  8.73 us
  transfers between devices with their start and end apart: 6, of which 5 were waited for; matrix products, arithmetic and copies ran while one was open for 27% of the time, Pallas kernels for 0%

commit v1 on v0

v1 whole, which is shorter than its diff:
```python
import functools

import jax
import jax.numpy as jnp
import numpy as np
from jax import lax
from jax.experimental import pallas as pl
from jax.experimental.pallas import tpu as pltpu
from jax.sharding import PartitionSpec as P

MESH = pl.DeviceIdType.MESH
HEAD = 128
GROUP = 4
D = 4096
TOK = 128
STRETCH = 1024
CACHE = 4096
STEPS = 4
ROWS = 4
QKV = (GROUP + 2) * HEAD
PIECE = 1024
EPSILON = 1e-05
THETA = 500000.0
NEG = -1e30
SCALE2 = float(HEAD ** (-0.5) * np.log2(np.e))

f32 = jnp.float32
bf16 = jnp.bfloat16


def tables():
    half = HEAD // 2
    freqs = (THETA ** (-np.arange(half, dtype=np.float64) / half)).astype(np.float32)
    angles = np.arange(STRETCH, dtype=np.float32)[:, None] * freqs
    cosine = np.cos(angles.astype(np.float64)).astype(np.float32)
    sine = np.sin(angles.astype(np.float64)).astype(np.float32)
    ct = np.concatenate([cosine, cosine], axis=1)
    st = np.concatenate([-sine, sine], axis=1)
    fr = np.broadcast_to(np.concatenate([freqs, freqs])[None, :], (8, HEAD))
    return ct, st, np.ascontiguousarray(fr)


def dot(a, b):
    return jnp.dot(a, b, preferred_element_type=f32)


def dot_t(a, b):
    return lax.dot_general(a, b, (((1,), (1,)), ((), ())), preferred_element_type=f32)


def kernel(
    plen_ref, assign_ref, slot_ref, clen_ref, gain_ref, freq_ref,
    prompt_ref, dec_ref, ck_ref, cv_ref, wqkv_ref, wout_ref, ct_ref, st_ref,
    out_ref, dout_ref,
    xp, xs, wq, wo, ck, cv, acc, qs, kv, at, pb, fr, nr, ct, st, ob, bias,
    dmv, x16, xd, qd, kd, vd, qr, ms, ls, os_, plt, pls, qnew, qn, pks, pk, od, dsb, drb, dfb, o32,
    lsem, outS, agS, agR, wS, wR, plS, plR, qnS, qnR, pkS, pkR, kvS, kvR, fS, fR, nS, nR, dS, dR, eS, eR,
):
    me = lax.axis_index("blk")
    pool = lax.axis_index("pool")
    batch = lax.axis_index("batch")
    x = me // 2
    c = lax.rem(me, 2)

    def near(dx, dc):
        return {"blk": lax.rem(x + dx + 4, 4) * 2 + lax.rem(c + dc, 2)}

    def other(j):
        return {"pool": 1 - pool, "batch": j}

    def peer(j):
        return {"blk": lax.rem(me + j, 8)}

    def remote(src, dst, ss, rs, dev):
        return pltpu.make_async_remote_copy(
            src_ref=src, dst_ref=dst, send_sem=ss, recv_sem=rs, device_id=dev, device_id_type=MESH
        )

    local = [
        pltpu.make_async_copy(prompt_ref.at[0], xp, lsem.at[0]),
        pltpu.make_async_copy(dec_ref, dmv, lsem.at[1]),
    ]
    for q in range(4):
        rows = pl.ds(q * PIECE, PIECE)
        local.append(pltpu.make_async_copy(wqkv_ref.at[rows], wq.at[0, rows], lsem.at[2 + q]))
    local.append(pltpu.make_async_copy(ct_ref, ct, lsem.at[6]))
    local.append(pltpu.make_async_copy(st_ref, st, lsem.at[7]))
    local.append(pltpu.make_async_copy(ck_ref, ck, lsem.at[8]))
    local.append(pltpu.make_async_copy(cv_ref, cv, lsem.at[9]))
    local.append(pltpu.make_async_copy(wout_ref, wo.at[0], lsem.at[10]))
    for cp in local:
        cp.start()

    barrier = pltpu.get_barrier_semaphore()
    for j in range(1, 8):
        pl.semaphore_signal(barrier, inc=1, device_id=peer(j), device_id_type=MESH)
    for j in range(8):
        pl.semaphore_signal(barrier, inc=1, device_id=other(j), device_id_type=MESH)

    plt[...] = jnp.full((8, 128), plen_ref[0, 0], jnp.int32)
    col = lax.broadcasted_iota(jnp.int32, (8, STRETCH), 1)
    bias[...] = jnp.where(col < jnp.full((8, STRETCH), plen_ref[0, 0], jnp.int32), 0.0, NEG)

    local[0].wait()

    def norm_band(i, _):
        rows = pl.ds(pl.multiple_of(i * 16, 16), 16)
        wide = xp[rows, :].astype(f32)
        factor = lax.rsqrt(jnp.mean(wide * wide, axis=-1, keepdims=True) + EPSILON)
        normed = (wide * factor * gain_ref[...]).astype(bf16)
        for q in range(4):
            xs[0, q, rows, :] = normed[:, q * PIECE:(q + 1) * PIECE]
        return 0

    lax.fori_loop(0, TOK // 16, norm_band, 0)
    pl.semaphore_wait(barrier, 15)

    def gather(direction, k):
        if direction == 0:
            if k < 4:
                return remote(xs.at[0, k], xs.at[1, k], agS.at[0, k], agR.at[0, k], near(1, 0))
            return remote(xs.at[1, k - 4], xs.at[3, k - 4], agS.at[0, k], agR.at[2, k - 4], near(1, 0))
        if k < 4:
            q = (k + 2) % 4
            return remote(xs.at[0, q], xs.at[2, q], agS.at[1, k], agR.at[1, q], near(-1, 0))
        return remote(xs.at[2, k - 2], xs.at[3, k - 2], agS.at[1, k], agR.at[2, k - 2], near(-1, 0))

    for k in range(4):
        gather(0, k).start()
        gather(1, k).start()

    def weight(k):
        if k < 4:
            rows = pl.ds(k * PIECE, PIECE)
            return remote(wqkv_ref.at[rows], wq.at[1, rows], wS.at[k], wR.at[k], near(0, 1))
        return remote(wout_ref, wo.at[1], wS.at[4], wR.at[4], near(0, 1))

    for k in range(5):
        weight(k).start()

    def length(j):
        return remote(plt, pls.at[batch], plS.at[j], plR.at[batch], other(j))

    for j in range(8):
        length(j).start()

    local[1].wait()
    for s in range(STEPS):
        x16[pl.ds(s * ROWS, ROWS), :] = dmv[s].astype(f32)
    wide = x16[...]
    factor = lax.rsqrt(jnp.mean(wide * wide, axis=-1, keepdims=True) + EPSILON)
    xd[...] = (wide * factor * gain_ref[...]).astype(bf16)
    joined = jnp.zeros((16, QKV), f32)
    for q in range(4):
        local[2 + q].wait()
        joined = joined + dot(xd[:, q * PIECE:(q + 1) * PIECE], wq[0, pl.ds(q * PIECE, PIECE), :])

    wanted = jnp.full((8, 128), assign_ref[0, 0], jnp.int32)
    newlen = jnp.zeros((8, 128), jnp.int32)
    for j in range(8):
        remote(plt, pls.at[j], plS.at[j], plR.at[j], other(j)).wait_recv()
    for j in range(8):
        newlen = newlen + jnp.where(wanted == j, pls[j], 0)
    row = lax.broadcasted_iota(jnp.int32, (16, 128), 0)
    row_r = lax.rem(row, ROWS)
    place = jnp.zeros((16, 128), jnp.int32)
    for r in range(ROWS):
        place = jnp.where(row_r == r, jnp.full((16, 128), clen_ref[r], jnp.int32), place)
    fresh = row_r == jnp.full((16, 128), slot_ref[0, 0], jnp.int32)
    place = jnp.where(fresh, jnp.broadcast_to(newlen[0:1, :], (16, 128)), place) + row // ROWS
    angle = place.astype(f32) * freq_ref[0:1, :]
    lane = lax.broadcasted_iota(jnp.int32, (16, 128), 1)
    dcos = jnp.cos(angle)
    dsin = jnp.sin(angle)
    dsin = jnp.where(lane < HEAD // 2, -dsin, dsin)

    def turn(u, cosine, sine):
        return u * cosine + pltpu.roll(u, HEAD // 2, 1) * sine

    for h in range(GROUP):
        qd[pl.ds(h * 16, 16), :] = turn(joined[:, h * HEAD:(h + 1) * HEAD], dcos, dsin)
    kd[...] = turn(joined[:, GROUP * HEAD:(GROUP + 1) * HEAD], dcos, dsin).astype(bf16)
    vd[...] = joined[:, (GROUP + 1) * HEAD:].astype(bf16)
    slots = jnp.full((16, 128), slot_ref[0, 0], jnp.int32)
    picked = jnp.zeros((16, 128), f32)
    for r in range(ROWS):
        part = qd[pl.ds(r, 16, stride=ROWS), :]
        qr[r] = part.astype(bf16)
        picked = picked + jnp.where(slots == r, part, 0.0)
    qnew[...] = picked.astype(bf16)

    def project(slot, q, a):
        tokens = xs[slot, q]
        rows = pl.ds(pl.multiple_of(q * PIECE, PIECE), PIECE)
        for h in range(2):
            acc[a, h] += dot(tokens, wq[h, rows, :])

    def origin(slot):
        return lax.rem(x + (0, 3, 1, 2)[slot], 4)

    def exchange(slot, h):
        rows = pl.ds(pl.multiple_of((origin(slot) * 2 + c) * TOK, TOK), TOK)
        return remote(kv.at[h, :, rows], kv.at[1 - h, :, rows], kvS.at[slot, h], kvR.at[slot, 1 - h], near(0, 1))

    def exchanged(slot, h):
        rows = pl.ds(pl.multiple_of((origin(slot) * 2 + 1 - c) * TOK, TOK), TOK)
        return remote(kv.at[h, :, rows], kv.at[h, :, rows], kvS.at[slot, h], kvR.at[slot, h], near(0, 1))

    def finish(slot, a):
        rows = pl.ds(pl.multiple_of((origin(slot) * 2 + c) * TOK, TOK), TOK)
        cosine = ct[rows, :]
        sine = st[rows, :]
        for h in range(2):
            kv[h, 0, rows, :] = turn(acc[a, h, :, GROUP * HEAD:(GROUP + 1) * HEAD], cosine, sine).astype(bf16)
            kv[h, 1, rows, :] = acc[a, h, :, (GROUP + 1) * HEAD:].astype(bf16)
        for h in range(2):
            for g in range(GROUP):
                qs[slot, h * GROUP + g] = turn(acc[a, h, :, g * HEAD:(g + 1) * HEAD], cosine, sine).astype(bf16)
        for h in range(2):
            exchange(slot, h).start()

    for k in range(4):
        weight(k).wait_recv()
    local[6].wait()
    local[7].wait()
    acc[0] = jnp.zeros((2, TOK, QKV), f32)
    lax.fori_loop(0, 4, lambda q, _: (project(0, q, 0), 0)[1], 0)

    def query(j):
        return remote(qnew, qn.at[batch], qnS.at[j], qnR.at[batch], other(j))

    for j in range(8):
        query(j).start()
    finish(0, 0)

    local[8].wait()
    local[9].wait()

    def old_row(r):
        q16 = qr[r]
        edge = jnp.full((16, CACHE), clen_ref[r], jnp.int32)
        edge = jnp.where(jnp.full((16, CACHE), slot_ref[0, 0], jnp.int32) == r, 0, edge)
        span = lax.broadcasted_iota(jnp.int32, (16, CACHE), 1)
        old = jnp.where(span < edge, dot_t(q16, ck[r]) * SCALE2, NEG)
        own = dot_t(q16, kd[...]) * SCALE2
        i16 = lax.broadcasted_iota(jnp.int32, (16, 16), 0)
        j16 = lax.broadcasted_iota(jnp.int32, (16, 16), 1)
        keep = (lax.rem(j16, ROWS) == r) & (j16 // ROWS <= lax.rem(i16, STEPS))
        own = jnp.where(keep, own, NEG)
        top = jnp.maximum(jnp.max(old, axis=-1, keepdims=True), jnp.max(own, axis=-1, keepdims=True))
        pold = jnp.exp2(old - top)
        pown = jnp.exp2(own - top)
        total = jnp.sum(pold, axis=-1, keepdims=True) + jnp.sum(pown, axis=-1, keepdims=True)
        mixed = dot(pold.astype(bf16), cv[r]) + dot(pown.astype(bf16), vd[...])
        ms[r] = jnp.broadcast_to(top, (16, 128))
        ls[r] = jnp.broadcast_to(total, (16, 128))
        os_[r] = mixed

    acc[0] = jnp.zeros((2, TOK, QKV), f32)
    acc[1] = jnp.zeros((2, TOK, QKV), f32)

    def near_step(t, _):
        q1 = t
        q2 = lax.rem(t + 2, 4)
        remote(xs.at[1, q1], xs.at[1, q1], agS.at[0, q1], agR.at[0, q1], near(1, 0)).wait_recv()
        remote(xs.at[2, q2], xs.at[2, q2], agS.at[1, q2], agR.at[1, q2], near(1, 0)).wait_recv()

        @pl.when(t < 2)
        def _():
            remote(xs.at[1, q1], xs.at[3, q1], agS.at[0, 4 + t], agR.at[2, q1], near(1, 0)).start()
            remote(xs.at[2, q2], xs.at[3, q2], agS.at[1, 4 + t], agR.at[2, q2], near(-1, 0)).start()

        project(1, q1, 0)
        project(2, q2, 1)
        old_row(t)
        return 0

    lax.fori_loop(0, 4, near_step, 0)
    finish(1, 0)
    finish(2, 1)

    acc[0] = jnp.zeros((2, TOK, QKV), f32)

    def far_step(t, _):
        for q in (t, t + 2):
            remote(xs.at[3, q], xs.at[3, q], agS.at[0, q], agR.at[2, q], near(1, 0)).wait_recv()
            project(3, q, 0)
        return 0

    lax.fori_loop(0, 2, far_step, 0)
    finish(3, 0)
    local[10].wait()
    weight(4).wait_recv()
    for slot in range(4):
        for h in range(2):
            exchanged(slot, h).wait_recv()

    def attend(d, X):
        for n in range(4):
            @pl.when(X == n)
            def _(n=n):
                size = 256 * (n + 1)

                def pair(hp, _):
                    q2 = qs[d, pl.ds(hp * 2, 2)].reshape(2 * TOK, HEAD)
                    h = hp // 2
                    s = dot_t(q2, kv[h, 0, pl.ds(0, size), :]) * SCALE2 + bias[0:1, :size]
                    last = s[:, size - 256:]
                    qi = lax.rem(lax.broadcasted_iota(jnp.int32, (2 * TOK, 256), 0), TOK) + c * TOK
                    ki = lax.broadcasted_iota(jnp.int32, (2 * TOK, 256), 1)
                    last = jnp.where(ki <= qi, last, NEG)
                    s = jnp.concatenate([s[:, :size - 256], last], axis=1) if n else last
                    top = jnp.max(s, axis=-1, keepdims=True)
                    p = jnp.exp2(s - top)
                    total = jnp.sum(p, axis=-1, keepdims=True)
                    o = dot(p.astype(bf16), kv[h, 1, pl.ds(0, size), :]) / total
                    o = o.astype(bf16)
                    at[:, pl.ds(pl.multiple_of(hp * 256, 256), HEAD)] = o[:TOK]
                    at[:, pl.ds(pl.multiple_of(hp * 256 + HEAD, HEAD), HEAD)] = o[TOK:]
                    return 0

                lax.fori_loop(0, 4, pair, 0)

    def out_piece(d, q):
        cols = pl.ds(pl.multiple_of(q * PIECE, PIECE), PIECE)
        part = dot(at[:, :512], wo[0, :, cols]) + dot(at[:, 512:], wo[1, :, cols])
        pb[d, q] = part.astype(bf16)

    def far_send(q):
        if q < 2:
            return remote(pb.at[3, q], fr.at[0, q], fS.at[0, q], fR.at[0, q], near(1, 0))
        return remote(pb.at[3, q], fr.at[1, q - 2], fS.at[1, q - 2], fR.at[1, q - 2], near(-1, 0))

    def near_send(direction, q):
        return remote(
            pb.at[2 - direction, q], nr.at[direction, q], nS.at[direction, q], nR.at[direction, q],
            near(1 - 2 * direction, 0),
        )

    def answer():
        for j in range(8):
            remote(qnew, qn.at[j], qnS.at[j], qnR.at[j], other(j)).wait_recv()
        q = qn[...].reshape(8 * 16, HEAD)
        s = dot_t(q, kv[0, 0]) * SCALE2 + bias[0:1, :]
        top = jnp.max(s, axis=-1, keepdims=True)
        p = jnp.exp2(s - top)
        total = jnp.sum(p, axis=-1, keepdims=True)
        o = dot(p.astype(bf16), kv[0, 1])
        pks[:, 0] = o.reshape(8, 16, HEAD)
        pks[:, 1] = jnp.broadcast_to(top, (128, HEAD)).reshape(8, 16, HEAD)
        pks[:, 2] = jnp.broadcast_to(total, (128, HEAD)).reshape(8, 16, HEAD)

    def reply(j):
        return remote(pks.at[j], pk.at[batch], pkS.at[j], pkR.at[batch], other(j))

    def block(t, _):
        d = 3 - t
        X = lax.rem(x + jnp.where(d == 3, 2, jnp.where(d == 2, 1, jnp.where(d == 1, 3, 0))), 4)
        attend(d, X)

        def piece(k, _):
            out_piece(d, lax.rem(k, 2) * 2 + k // 2)
            return 0

        lax.fori_loop(0, 4, piece, 0)

        @pl.when(t == 0)
        def _():
            for q in (0, 2, 1, 3):
                far_send(q).start()
            answer()

        @pl.when(t == 1)
        def _():
            for j in range(8):
                reply(j).start()
            for q in (2, 3):
                near_send(0, q).start()

        @pl.when(t == 2)
        def _():
            for q in (0, 1):
                near_send(1, q).start()

        return 0

    lax.fori_loop(0, 4, block, 0)

    for j in range(8):
        remote(pks.at[j], pk.at[j], pkS.at[j], pkR.at[j], other(j)).wait_recv()
    want = jnp.full((16, 128), assign_ref[0, 0], jnp.int32)
    no = jnp.zeros((16, 128), f32)
    nm = jnp.zeros((16, 128), f32)
    nl = jnp.zeros((16, 128), f32)
    for j in range(8):
        hit = want == j
        no = no + jnp.where(hit, pk[j, 0], 0.0)
        nm = nm + jnp.where(hit, pk[j, 1], 0.0)
        nl = nl + jnp.where(hit, pk[j, 2], 0.0)
    for r in range(ROWS):
        mine = slots == r
        m2 = jnp.where(mine, nm, NEG)
        top = jnp.maximum(ms[r], m2)
        a = jnp.exp2(ms[r] - top)
        b = jnp.exp2(m2 - top)
        o = (os_[r] * a + no * b) / (ls[r] * a + nl * b)
        od[pl.ds(r, 16, stride=ROWS), :] = o
    part = jnp.zeros((16, D), f32)
    for h in range(GROUP):
        part = part + dot(od[pl.ds(h * 16, 16), :].astype(bf16), wo[0, pl.ds(h * HEAD, HEAD), :])
    for k in range(8):
        dsb[k] = part[:, k * 512:(k + 1) * 512].astype(bf16)

    def scatter(j):
        return remote(dsb.at[lax.rem(me + j, 8)], drb.at[j - 1], dS.at[j - 1], dR.at[j - 1], peer(j))

    for j in range(1, 8):
        scatter(j).start()

    for q in (0, 1):
        far_send(q).wait_recv()
        pb[2, q] = (pb[2, q].astype(f32) + fr[0, q].astype(f32)).astype(bf16)
        far_send(q + 2).wait_recv()
        pb[1, q + 2] = (pb[1, q + 2].astype(f32) + fr[1, q].astype(f32)).astype(bf16)
        near_send(0, q).start()
        near_send(1, q + 2).start()

    for j in range(1, 8):
        scatter(j).wait_recv()
    mycols = pl.ds(pl.multiple_of(me * 512, 512), 512)
    total = dsb[me].astype(f32)
    for j in range(7):
        total = total + drb[j].astype(f32)
    done = (x16[:, mycols] + total).astype(bf16)
    dfb[0] = done
    o32[:, mycols] = done.astype(f32)

    def spread(j):
        return remote(dfb.at[0], dfb.at[j], eS.at[j - 1], eR.at[j - 1], peer(j))

    for j in range(1, 8):
        spread(j).start()

    outs = []
    for i, q in enumerate((0, 2, 1, 3)):
        near_send(0, q).wait_recv()
        near_send(1, q).wait_recv()
        cols = slice(q * PIECE, (q + 1) * PIECE)
        total = pb[0, q].astype(f32) + nr[0, q].astype(f32) + nr[1, q].astype(f32)
        ob[:, cols] = (xp[:, cols].astype(f32) + total).astype(bf16)
        cp = pltpu.make_async_copy(ob.at[:, cols], out_ref.at[0, :, cols], outS.at[q])
        cp.start()
        outs.append(cp)

    for j in range(1, 8):
        spread(j).wait_recv()
    for j in range(1, 8):
        cols = pl.ds(pl.multiple_of(lax.rem(me - j + 8, 8) * 512, 512), 512)
        o32[:, cols] = dfb[j].astype(f32)
    for s in range(STEPS):
        dout_ref[s] = o32[pl.ds(s * ROWS, ROWS), :].astype(bf16)

    for k in range(6):
        gather(0, k).wait_send()
        gather(1, k).wait_send()
    for k in range(5):
        weight(k).wait_send()
    for j in range(8):
        length(j).wait_send()
        query(j).wait_send()
        reply(j).wait_send()
    for slot in range(4):
        for h in range(2):
            exchange(slot, h).wait_send()
    for q in range(4):
        far_send(q).wait_send()
        near_send(0, q).wait_send()
        near_send(1, q).wait_send()
    for j in range(1, 8):
        scatter(j).wait_send()
        spread(j).wait_send()
    for cp in outs:
        cp.wait()


def body(
    prompt, prompt_len, dec_tokens, cache_k, cache_v, cache_len, assign, slot, gain, w_qkv, w_out
):
    ct, st, fr = tables()
    any_ = pl.BlockSpec(memory_space=pl.ANY)
    smem = pl.BlockSpec(memory_space=pltpu.SMEM)
    vmem = pl.BlockSpec(memory_space=pltpu.VMEM)
    V = pltpu.VMEM
    dma = pltpu.SemaphoreType.DMA
    return pl.pallas_call(
        kernel,
        out_shape=(
            jax.ShapeDtypeStruct((1, TOK, D), bf16),
            jax.ShapeDtypeStruct((STEPS, ROWS, D), bf16),
        ),
        in_specs=[smem] * 4 + [vmem] * 2 + [any_] * 8,
        out_specs=(any_, vmem),
        scratch_shapes=[
            V((TOK, D), bf16),
            V((4, 4, TOK, PIECE), bf16),
            V((2, D, QKV), bf16),
            V((2, 512, D), bf16),
            V((ROWS, CACHE, HEAD), bf16),
            V((ROWS, CACHE, HEAD), bf16),
            V((2, 2, TOK, QKV), f32),
            V((4, 8, TOK, HEAD), bf16),
            V((2, 2, STRETCH, HEAD), bf16),
            V((TOK, 1024), bf16),
            V((4, 4, TOK, PIECE), bf16),
            V((2, 2, TOK, PIECE), bf16),
            V((2, 4, TOK, PIECE), bf16),
            V((STRETCH, HEAD), f32),
            V((STRETCH, HEAD), f32),
            V((TOK, D), bf16),
            V((8, STRETCH), f32),
            V((STEPS, ROWS, D), bf16),
            V((16, D), f32),
            V((16, D), bf16),
            V((64, HEAD), f32),
            V((16, HEAD), bf16),
            V((16, HEAD), bf16),
            V((ROWS, 16, HEAD), bf16),
            V((ROWS, 16, HEAD), f32),
            V((ROWS, 16, HEAD), f32),
            V((ROWS, 16, HEAD), f32),
            V((8, 128), jnp.int32),
            V((8, 8, 128), jnp.int32),
            V((16, HEAD), bf16),
            V((8, 16, HEAD), bf16),
            V((8, 3, 16, HEAD), f32),
            V((8, 3, 16, HEAD), f32),
            V((64, HEAD), f32),
            V((8, 16, 512), bf16),
            V((7, 16, 512), bf16),
            V((8, 16, 512), bf16),
            V((16, D), f32),
            dma((11,)), dma((4,)),
            dma((2, 6)), dma((3, 4)),
            dma((5,)), dma((5,)),
            dma((8,)), dma((8,)),
            dma((8,)), dma((8,)),
            dma((8,)), dma((8,)),
            dma((4, 2)), dma((4, 2)),
            dma((2, 2)), dma((2, 2)),
            dma((2, 4)), dma((2, 4)),
            dma((7,)), dma((7,)),
            dma((7,)), dma((7,)),
        ],
        compiler_params=pltpu.CompilerParams(
            collective_id=0, has_side_effects=True, vmem_limit_bytes=61 * 2**20
        ),
        name="layer",
    )(
        prompt_len, assign, slot, cache_len, gain.reshape(1, D), jnp.asarray(fr),
        prompt, dec_tokens, cache_k, cache_v, w_qkv, w_out, jnp.asarray(ct), jnp.asarray(st),
    )


def solution(mesh):
    return jax.shard_map(
        body,
        mesh=mesh,
        in_specs=(
            P(("pool", "batch"), "blk", None),
            P("pool", "batch"),
            P(None, ("pool", "batch"), None),
            P(("pool", "batch"), None, "blk"),
            P(("pool", "batch"), None, "blk"),
            P(("pool", "batch")),
            P("pool", "batch"),
            P("pool", "batch"),
            P(),
            P(None, "blk"),
            P("blk", None),
        ),
        out_specs=(P(("pool", "batch"), "blk", None), P(None, ("pool", "batch"), None)),
        check_vma=False,
    )
```

time: 260 us -> 98.3 us (0.38)
  waiting for transfers between devices: 110 us -> 0 us
  Pallas kernels: 0 us -> 91.6 us
  matrix products: 39.9 us -> 0 us
  blocking collectives: 36.1 us -> 0 us
  other arithmetic: 28.8 us -> 0 us
  local copies, waits for them, and re-layouts: 21.6 us -> 3.89 us
  between operations: 16.1 us -> 2.58 us
  starting transfers between devices: 6.76 us -> 0 us
    pallas_call x0 -> x1, Pallas kernels: none -> 91.6 us  [body(): pl.pallas_call(kernel, out_shape=(jax.ShapeDtypeStruct((1, TOK, D), bf16)...]
    all_gather x2 -> x0, waiting for transfers between devices: 72.1 us -> none  [the longest x1 53.3 us: body(): lax.all_gather(normed, 'blk', axis=0, tiled=True)]
    dot_general x12 -> x0, matrix products: 39.9 us -> none  [the longest x1 11 us: body(): jnp.dot(lax.all_gather(normed, 'blk', axis=0, tiled=True), w_qkv, preferr...]
    reduce_scatter x1 -> x0, waiting for transfers between devices: 29.3 us -> none  [body(): lax.psum_scatter(jnp.dot(rows, w_out, preferred_element_type=f32).astype(...]
    all_to_all x1 -> x0, blocking collectives: 25.9 us -> none  [copy_for_each(): return lax.all_to_all(copies, axis, split_axis=0, concat_axis=0, tiled=True)]
    unnamed x32 -> x2, local copies, waits for them, and re-layouts: 18 us -> 3.89 us
    reduce_sum x7 -> x0, other arithmetic: 11.2 us -> none  [the longest x2 4.33 us: softmax_weights(): return (expo / jnp.sum(expo, axis=-1, keepdims=True)).astype(jnp.bfloat16)]
    unnamed x1 -> x0, blocking collectives: 10.2 us -> none
  transfers between devices with their start and end apart: 6 -> 0, of which waited for: 5 -> 0; matrix products, arithmetic and copies ran while one was open for 27% -> 0% of each run, Pallas kernels for 0% -> 0%
where the time goes in v1:
time: 98.3 us; the launch traced here: 98.1 us
  Pallas kernels  91.6 us (93%)
  local copies, waits for them, and re-layouts  3.89 us (4%)
  between operations  2.58 us (3%)
    pallas_call x1, Pallas kernels, body(): pl.pallas_call(kernel, out_shape=(jax.ShapeDtypeStruct((1, TOK, D), bf16)...  91.6 us
    unnamed x2, local copies, waits for them, and re-layouts  3.89 us

profile of v1, /device:TPU:1, one launch (start us, length us, event | category | flops | bytes accessed | tf_op | source)
XLA Modules:
  0.0 98.1 jit_solution(10105324299516150744)
XLA Ops:
  2.6 91.6 %layer.1 = (bf16[1,128,4096]{2,1,0:T(8,128)(2,1)}, bf16[4,4,4096]{2,1,0:T(4,128)(2,1)}) custom-call(s32[1,1]{1,0:T(1,128)S(6)} %copy.18.plen_ref, s32[1,1]{1,0:T(1,128)S(6)} %copy.19.assign_ref, s32[1,1]{1,0:T(1,128)S(6)} %copy.20.slot_ref, s32[4]{0:T(128)} %clen_ref.1, f32[1,4096]{1,0:T(1,128)} %bitcast.1, f32[8,128]{1,0:T(8,128)} %constant.6.clone.freq_ref, ...), custom_call_target="tpu_custom_call" | custom-call | tf_op jit(solution)/shard_map/layer/pallas_call | solution.py:495
  94.2 2.3 %copy.21 = bf16[1,128,4096]{2,1,0:T(8,128)(2,1)} copy(bf16[1,128,4096]{2,1,0:T(8,128)(2,1)} %get-tuple-element.4) | data formatting | bytes 2097152
  96.5 1.6 %copy.22 = bf16[4,4,4096]{2,1,0:T(4,128)(2,1)} copy(bf16[4,4,4096]{2,1,0:T(4,128)(2,1)} %get-tuple-element.5) | data formatting | bytes 262144

commit v2 on v1

--- a/solution.py
+++ b/solution.py
@@ -52,9 +52,9 @@
     plen_ref, assign_ref, slot_ref, clen_ref, gain_ref, freq_ref,
     prompt_ref, dec_ref, ck_ref, cv_ref, wqkv_ref, wout_ref, ct_ref, st_ref,
     out_ref, dout_ref,
-    xp, xs, wq, wo, ck, cv, acc, qs, kv, at, pb, fr, nr, ct, st, ob, bias,
-    dmv, x16, xd, qd, kd, vd, qr, ms, ls, os_, plt, pls, qnew, qn, pks, pk, od, dsb, drb, dfb, o32,
-    lsem, outS, agS, agR, wS, wR, plS, plR, qnS, qnR, pkS, pkR, kvS, kvR, fS, fR, nS, nR, dS, dR, eS, eR,
+    xs, wq, wo, ck, cv, acc, ssq, qs, kv, so, sm, sl, at, pb, fr, nr, ct, st, bias,
+    xn, dmv, x16, xd, qd, kd, vd, qr, ms, ls, os_, plt, pls, qnew, qn, pks, pk, od, dsb, drb, dfb, o32,
+    lsem, agS, agR, wS, wR, plS, plR, qnS, qnR, pkS, pkR, kvS, kvR, fS, fR, nS, nR, dS, dR, eS, eR,
 ):
     me = lax.axis_index("blk")
     pool = lax.axis_index("pool")
@@ -76,10 +76,7 @@
             src_ref=src, dst_ref=dst, send_sem=ss, recv_sem=rs, device_id=dev, device_id_type=MESH
         )
 
-    local = [
-        pltpu.make_async_copy(prompt_ref.at[0], xp, lsem.at[0]),
-        pltpu.make_async_copy(dec_ref, dmv, lsem.at[1]),
-    ]
+    local = [pltpu.make_async_copy(dec_ref, dmv, lsem.at[1])]
     for q in range(4):
         rows = pl.ds(q * PIECE, PIECE)
         local.append(pltpu.make_async_copy(wqkv_ref.at[rows], wq.at[0, rows], lsem.at[2 + q]))
@@ -88,6 +85,11 @@
     local.append(pltpu.make_async_copy(ck_ref, ck, lsem.at[8]))
     local.append(pltpu.make_async_copy(cv_ref, cv, lsem.at[9]))
     local.append(pltpu.make_async_copy(wout_ref, wo.at[0], lsem.at[10]))
+    for q in range(4):
+        local.insert(2 + 2 * q, pltpu.make_async_copy(prompt_ref.at[0, :, pl.ds(q * PIECE, PIECE)], xs.at[0, q], lsem.at[(0, 11, 12, 13)[q]]))
+    ldec, w0, t0, w1, t1, w2, t2, w3, t3, lct, lst, lck, lcv, lwo = local
+    lweights = (w0, w1, w2, w3)
+    ltokens = (t0, t1, t2, t3)
     for cp in local:
         cp.start()
 
@@ -101,28 +103,16 @@
     col = lax.broadcasted_iota(jnp.int32, (8, STRETCH), 1)
     bias[...] = jnp.where(col < jnp.full((8, STRETCH), plen_ref[0, 0], jnp.int32), 0.0, NEG)
 
-    local[0].wait()
-
-    def norm_band(i, _):
-        rows = pl.ds(pl.multiple_of(i * 16, 16), 16)
-        wide = xp[rows, :].astype(f32)
-        factor = lax.rsqrt(jnp.mean(wide * wide, axis=-1, keepdims=True) + EPSILON)
-        normed = (wide * factor * gain_ref[...]).astype(bf16)
-        for q in range(4):
-            xs[0, q, rows, :] = normed[:, q * PIECE:(q + 1) * PIECE]
-        return 0
-
-    lax.fori_loop(0, TOK // 16, norm_band, 0)
     pl.semaphore_wait(barrier, 15)
 
     def gather(direction, k):
         if direction == 0:
             if k < 4:
-                return remote(xs.at[0, k], xs.at[1, k], agS.at[0, k], agR.at[0, k], near(1, 0))
+                return remote(prompt_ref.at[0, :, pl.ds(k * PIECE, PIECE)], xs.at[1, k], agS.at[0, k], agR.at[0, k], near(1, 0))
             return remote(xs.at[1, k - 4], xs.at[3, k - 4], agS.at[0, k], agR.at[2, k - 4], near(1, 0))
         if k < 4:
             q = (k + 2) % 4
-            return remote(xs.at[0, q], xs.at[2, q], agS.at[1, k], agR.at[1, q], near(-1, 0))
+            return remote(prompt_ref.at[0, :, pl.ds(q * PIECE, PIECE)], xs.at[2, q], agS.at[1, k], agR.at[1, q], near(-1, 0))
         return remote(xs.at[2, k - 2], xs.at[3, k - 2], agS.at[1, k], agR.at[2, k - 2], near(-1, 0))
 
     for k in range(4):
@@ -144,7 +134,7 @@
     for j in range(8):
         length(j).start()
 
-    local[1].wait()
+    ldec.wait()
     for s in range(STEPS):
         x16[pl.ds(s * ROWS, ROWS), :] = dmv[s].astype(f32)
     wide = x16[...]
@@ -152,8 +142,39 @@
     xd[...] = (wide * factor * gain_ref[...]).astype(bf16)
     joined = jnp.zeros((16, QKV), f32)
     for q in range(4):
-        local[2 + q].wait()
+        lweights[q].wait()
         joined = joined + dot(xd[:, q * PIECE:(q + 1) * PIECE], wq[0, pl.ds(q * PIECE, PIECE), :])
+
+    def scaled(slot, q, a):
+        wide = xs[slot, q].astype(f32)
+        square = wide * wide
+        part = square[:, :HEAD]
+        for i in range(1, PIECE // HEAD):
+            part = part + square[:, i * HEAD:(i + 1) * HEAD]
+        ssq[a] += part
+        return (wide * gain_ref[:, pl.ds(pl.multiple_of(q * PIECE, PIECE), PIECE)]).astype(bf16)
+
+    def project(slot, q, a):
+        tokens = scaled(slot, q, a)
+        rows = pl.ds(pl.multiple_of(q * PIECE, PIECE), PIECE)
+        for h in range(2):
+            acc[a, h] += dot(tokens, wq[h, rows, :])
+
+    def clear(a):
+        acc[a] = jnp.zeros((2, TOK, QKV), f32)
+        ssq[a] = jnp.zeros((TOK, HEAD), f32)
+
+    clear(0)
+    for q in range(4):
+        ltokens[q].wait()
+
+    def own_first(q, _):
+        tokens = scaled(0, q, 0)
+        xn[q] = tokens
+        acc[0, 0] += dot(tokens, wq[0, pl.ds(pl.multiple_of(q * PIECE, PIECE), PIECE), :])
+        return 0
+
+    lax.fori_loop(0, 4, own_first, 0)
 
     wanted = jnp.full((8, 128), assign_ref[0, 0], jnp.int32)
     newlen = jnp.zeros((8, 128), jnp.int32)
@@ -189,14 +210,10 @@
         picked = picked + jnp.where(slots == r, part, 0.0)
     qnew[...] = picked.astype(bf16)
 
-    def project(slot, q, a):
-        tokens = xs[slot, q]
-        rows = pl.ds(pl.multiple_of(q * PIECE, PIECE), PIECE)
-        for h in range(2):
-            acc[a, h] += dot(tokens, wq[h, rows, :])
-
     def origin(slot):
-        return lax.rem(x + (0, 3, 1, 2)[slot], 4)
+        if isinstance(slot, int):
+            return lax.rem(x + (0, 3, 1, 2)[slot], 4)
+        return lax.rem(x + jnp.where(slot == 1, 3, jnp.where(slot == 2, 1, jnp.where(slot == 3, 2, 0))), 4)
 
     def exchange(slot, h):
         rows = pl.ds(pl.multiple_of((origin(slot) * 2 + c) * TOK, TOK), TOK)
@@ -208,33 +225,17 @@
 
     def finish(slot, a):
         rows = pl.ds(pl.multiple_of((origin(slot) * 2 + c) * TOK, TOK), TOK)
-        cosine = ct[rows, :]
-        sine = st[rows, :]
+        factor = lax.rsqrt(jnp.sum(ssq[a], axis=-1, keepdims=True) * (1.0 / D) + EPSILON)
+        cosine = ct[rows, :] * factor
+        sine = st[rows, :] * factor
         for h in range(2):
             kv[h, 0, rows, :] = turn(acc[a, h, :, GROUP * HEAD:(GROUP + 1) * HEAD], cosine, sine).astype(bf16)
-            kv[h, 1, rows, :] = acc[a, h, :, (GROUP + 1) * HEAD:].astype(bf16)
+            kv[h, 1, rows, :] = (acc[a, h, :, (GROUP + 1) * HEAD:] * factor).astype(bf16)
         for h in range(2):
             for g in range(GROUP):
                 qs[slot, h * GROUP + g] = turn(acc[a, h, :, g * HEAD:(g + 1) * HEAD], cosine, sine).astype(bf16)
         for h in range(2):
             exchange(slot, h).start()
-
-    for k in range(4):
-        weight(k).wait_recv()
-    local[6].wait()
-    local[7].wait()
-    acc[0] = jnp.zeros((2, TOK, QKV), f32)
-    lax.fori_loop(0, 4, lambda q, _: (project(0, q, 0), 0)[1], 0)
-
-    def query(j):
-        return remote(qnew, qn.at[batch], qnS.at[j], qnR.at[batch], other(j))
-
-    for j in range(8):
-        query(j).start()
-    finish(0, 0)
-
-    local[8].wait()
-    local[9].wait()
 
     def old_row(r):
         q16 = qr[r]
@@ -256,8 +257,33 @@
         ls[r] = jnp.broadcast_to(total, (16, 128))
         os_[r] = mixed
 
-    acc[0] = jnp.zeros((2, TOK, QKV), f32)
-    acc[1] = jnp.zeros((2, TOK, QKV), f32)
+    def query(j):
+        return remote(qnew, qn.at[batch], qnS.at[j], qnR.at[batch], other(j))
+
+    lck.wait()
+    lcv.wait()
+
+    def early_row(r, _):
+        old_row(r)
+        return 0
+
+    lax.fori_loop(0, 2, early_row, 0)
+    for j in range(8):
+        query(j).start()
+    for k in range(4):
+        weight(k).wait_recv()
+    lct.wait()
+    lst.wait()
+
+    def own_second(q, _):
+        acc[0, 1] += dot(xn[q], wq[1, pl.ds(pl.multiple_of(q * PIECE, PIECE), PIECE), :])
+        return 0
+
+    lax.fori_loop(0, 4, own_second, 0)
+    finish(0, 0)
+
+    clear(0)
+    clear(1)
 
     def near_step(t, _):
         q1 = t
@@ -272,14 +298,78 @@
 
         project(1, q1, 0)
         project(2, q2, 1)
-        old_row(t)
+
+        @pl.when(t < 2)
+        def _():
+            old_row(t + 2)
+
         return 0
 
     lax.fori_loop(0, 4, near_step, 0)
     finish(1, 0)
     finish(2, 1)
 
-    acc[0] = jnp.zeros((2, TOK, QKV), f32)
+    def attend_own(d):
+        krows = pl.ds(pl.multiple_of(origin(d) * 256, 256), 256)
+
+        def pair(hp, _):
+            q2 = qs[d, pl.ds(hp * 2, 2)].reshape(2 * TOK, HEAD)
+            h = hp // 2
+            s = dot_t(q2, kv[h, 0, krows, :]) * SCALE2 + bias[0:1, krows]
+            qi = lax.rem(lax.broadcasted_iota(jnp.int32, (2 * TOK, 256), 0), TOK) + c * TOK
+            ki = lax.broadcasted_iota(jnp.int32, (2 * TOK, 256), 1)
+            s = jnp.where(ki <= qi, s, NEG)
+            top = jnp.max(s, axis=-1, keepdims=True)
+            p = jnp.exp2(s - top)
+            sm[d, hp] = jnp.broadcast_to(top, (2 * TOK, HEAD))
+            sl[d, hp] = jnp.broadcast_to(jnp.sum(p, axis=-1, keepdims=True), (2 * TOK, HEAD))
+            so[d, hp] = dot(p.astype(bf16), kv[h, 1, krows, :])
+            return 0
+
+        lax.fori_loop(0, 4, pair, 0)
+
+    def attend_more(d, k):
+        krows = pl.ds(pl.multiple_of(origin(k) * 256, 256), 256)
+
+        def pair(hp, _):
+            q2 = qs[d, pl.ds(hp * 2, 2)].reshape(2 * TOK, HEAD)
+            h = hp // 2
+            s = dot_t(q2, kv[h, 0, krows, :]) * SCALE2 + bias[0:1, krows]
+            before = sm[d, hp]
+            top = jnp.maximum(before, jnp.broadcast_to(jnp.max(s, axis=-1, keepdims=True), (2 * TOK, HEAD)))
+            p = jnp.exp2(s - jnp.concatenate([top, top], axis=1))
+            fade = jnp.exp2(before - top)
+            sm[d, hp] = top
+            sl[d, hp] = sl[d, hp] * fade + jnp.broadcast_to(jnp.sum(p, axis=-1, keepdims=True), (2 * TOK, HEAD))
+            so[d, hp] = so[d, hp] * fade + dot(p.astype(bf16), kv[h, 1, krows, :])
+            return 0
+
+        @pl.when(origin(k) < origin(d))
+        def _():
+            lax.fori_loop(0, 4, pair, 0)
+
+    def attend_near(d):
+        attend_own(d)
+        for i in (1, 2) if not isinstance(d, int) else ():
+            attend_more(d, lax.rem(d + i, 3))
+
+    def settle(d):
+        for hp in range(4):
+            o = (so[d, hp] / sl[d, hp]).astype(bf16)
+            at[d, :, hp * 256:hp * 256 + HEAD] = o[:TOK]
+            at[d, :, hp * 256 + HEAD:(hp + 1) * 256] = o[TOK:]
+
+    for slot in range(3):
+        for h in range(2):
+            exchanged(slot, h).wait_recv()
+
+    def before_far(i, _):
+        attend_near(lax.rem(i + 1, 3))
+        return 0
+
+    lax.fori_loop(0, 3, before_far, 0)
+
+    clear(0)
 
     def far_step(t, _):
         for q in (t, t + 2):
@@ -289,41 +379,14 @@
 
     lax.fori_loop(0, 2, far_step, 0)
     finish(3, 0)
-    local[10].wait()
+    lwo.wait()
     weight(4).wait_recv()
-    for slot in range(4):
-        for h in range(2):
-            exchanged(slot, h).wait_recv()
-
-    def attend(d, X):
-        for n in range(4):
-            @pl.when(X == n)
-            def _(n=n):
-                size = 256 * (n + 1)
-
-                def pair(hp, _):
-                    q2 = qs[d, pl.ds(hp * 2, 2)].reshape(2 * TOK, HEAD)
-                    h = hp // 2
-                    s = dot_t(q2, kv[h, 0, pl.ds(0, size), :]) * SCALE2 + bias[0:1, :size]
-                    last = s[:, size - 256:]
-                    qi = lax.rem(lax.broadcasted_iota(jnp.int32, (2 * TOK, 256), 0), TOK) + c * TOK
-                    ki = lax.broadcasted_iota(jnp.int32, (2 * TOK, 256), 1)
-                    last = jnp.where(ki <= qi, last, NEG)
-                    s = jnp.concatenate([s[:, :size - 256], last], axis=1) if n else last
-                    top = jnp.max(s, axis=-1, keepdims=True)
-                    p = jnp.exp2(s - top)
-                    total = jnp.sum(p, axis=-1, keepdims=True)
-                    o = dot(p.astype(bf16), kv[h, 1, pl.ds(0, size), :]) / total
-                    o = o.astype(bf16)
-                    at[:, pl.ds(pl.multiple_of(hp * 256, 256), HEAD)] = o[:TOK]
-                    at[:, pl.ds(pl.multiple_of(hp * 256 + HEAD, HEAD), HEAD)] = o[TOK:]
-                    return 0
-
-                lax.fori_loop(0, 4, pair, 0)
+    for h in range(2):
+        exchanged(3, h).wait_recv()
 
     def out_piece(d, q):
         cols = pl.ds(pl.multiple_of(q * PIECE, PIECE), PIECE)
-        part = dot(at[:, :512], wo[0, :, cols]) + dot(at[:, 512:], wo[1, :, cols])
+        part = dot(at[d, :, :512], wo[0, :, cols]) + dot(at[d, :, 512:], wo[1, :, cols])
         pb[d, q] = part.astype(bf16)
 
     def far_send(q):
@@ -353,38 +416,41 @@
     def reply(j):
         return remote(pks.at[j], pk.at[batch], pkS.at[j], pkR.at[batch], other(j))
 
-    def block(t, _):
-        d = 3 - t
-        X = lax.rem(x + jnp.where(d == 3, 2, jnp.where(d == 2, 1, jnp.where(d == 1, 3, 0))), 4)
-        attend(d, X)
-
+    def pieces(d, first, second):
         def piece(k, _):
-            out_piece(d, lax.rem(k, 2) * 2 + k // 2)
+            out_piece(d, jnp.where(k == 0, first, second))
             return 0
 
-        lax.fori_loop(0, 4, piece, 0)
-
-        @pl.when(t == 0)
-        def _():
-            for q in (0, 2, 1, 3):
-                far_send(q).start()
-            answer()
-
-        @pl.when(t == 1)
-        def _():
-            for j in range(8):
-                reply(j).start()
-            for q in (2, 3):
-                near_send(0, q).start()
-
-        @pl.when(t == 2)
-        def _():
-            for q in (0, 1):
-                near_send(1, q).start()
-
+        lax.fori_loop(0, 2, piece, 0)
+
+    attend_more(2, 3)
+    settle(2)
+    pieces(2, 2, 3)
+    near_send(0, 2).start()
+    near_send(0, 3).start()
+    attend_more(1, 3)
+    settle(1)
+    pieces(1, 0, 1)
+    near_send(1, 0).start()
+    near_send(1, 1).start()
+    answer()
+
+    attend_own(3)
+
+    def far_keys(k, _):
+        attend_more(3, k)
         return 0
 
-    lax.fori_loop(0, 4, block, 0)
+    lax.fori_loop(0, 3, far_keys, 0)
+    for j in range(8):
+        reply(j).start()
+    settle(3)
+    pieces(3, 0, 2)
+    far_send(0).start()
+    far_send(2).start()
+    pieces(3, 1, 3)
+    far_send(1).start()
+    far_send(3).start()
 
     for j in range(8):
         remote(pks.at[j], pk.at[j], pkS.at[j], pkR.at[j], other(j)).wait_recv()
@@ -417,13 +483,12 @@
     for j in range(1, 8):
         scatter(j).start()
 
-    for q in (0, 1):
-        far_send(q).wait_recv()
-        pb[2, q] = (pb[2, q].astype(f32) + fr[0, q].astype(f32)).astype(bf16)
-        far_send(q + 2).wait_recv()
-        pb[1, q + 2] = (pb[1, q + 2].astype(f32) + fr[1, q].astype(f32)).astype(bf16)
-        near_send(0, q).start()
-        near_send(1, q + 2).start()
+    pieces(2, 0, 1)
+    pieces(1, 2, 3)
+    attend_more(0, 3)
+    settle(0)
+    pieces(0, 0, 2)
+    pieces(0, 1, 3)
 
     for j in range(1, 8):
         scatter(j).wait_recv()
@@ -441,24 +506,29 @@
     for j in range(1, 8):
         spread(j).start()
 
-    outs = []
+    def relay(q):
+        far_send(q).wait_recv()
+        pb[2, q] = (pb[2, q].astype(f32) + fr[0, q].astype(f32)).astype(bf16)
+        far_send(q + 2).wait_recv()
+        pb[1, q + 2] = (pb[1, q + 2].astype(f32) + fr[1, q].astype(f32)).astype(bf16)
+        near_send(0, q).start()
+        near_send(1, q + 2).start()
+
+    relay(0)
+    for j in range(1, 8):
+        spread(j).wait_recv()
+    for j in range(1, 8):
+        cols = pl.ds(pl.multiple_of(lax.rem(me - j + 8, 8) * 512, 512), 512)
+        o32[:, cols] = dfb[j].astype(f32)
+    dout_ref[...] = o32[...].astype(bf16)
+    relay(1)
+
     for i, q in enumerate((0, 2, 1, 3)):
         near_send(0, q).wait_recv()
         near_send(1, q).wait_recv()
         cols = slice(q * PIECE, (q + 1) * PIECE)
         total = pb[0, q].astype(f32) + nr[0, q].astype(f32) + nr[1, q].astype(f32)
-        ob[:, cols] = (xp[:, cols].astype(f32) + total).astype(bf16)
-        cp = pltpu.make_async_copy(ob.at[:, cols], out_ref.at[0, :, cols], outS.at[q])
-        cp.start()
-        outs.append(cp)
-
-    for j in range(1, 8):
-        spread(j).wait_recv()
-    for j in range(1, 8):
-        cols = pl.ds(pl.multiple_of(lax.rem(me - j + 8, 8) * 512, 512), 512)
-        o32[:, cols] = dfb[j].astype(f32)
-    for s in range(STEPS):
-        dout_ref[s] = o32[pl.ds(s * ROWS, ROWS), :].astype(bf16)
+        out_ref[:, cols] = (xs[0, q].astype(f32) + total).astype(bf16)
 
     for k in range(6):
         gather(0, k).wait_send()
@@ -479,8 +549,6 @@
     for j in range(1, 8):
         scatter(j).wait_send()
         spread(j).wait_send()
-    for cp in outs:
-        cp.wait()
 
 
 def body(
@@ -492,32 +560,36 @@
     vmem = pl.BlockSpec(memory_space=pltpu.VMEM)
     V = pltpu.VMEM
     dma = pltpu.SemaphoreType.DMA
-    return pl.pallas_call(
+    OUT = pltpu.VMEM
+    out, dout = pl.pallas_call(
         kernel,
         out_shape=(
-            jax.ShapeDtypeStruct((1, TOK, D), bf16),
-            jax.ShapeDtypeStruct((STEPS, ROWS, D), bf16),
+            OUT((TOK, D), bf16),
+            OUT((16, D), bf16),
         ),
         in_specs=[smem] * 4 + [vmem] * 2 + [any_] * 8,
-        out_specs=(any_, vmem),
+        out_specs=(vmem, vmem),
         scratch_shapes=[
-            V((TOK, D), bf16),
             V((4, 4, TOK, PIECE), bf16),
             V((2, D, QKV), bf16),
             V((2, 512, D), bf16),
             V((ROWS, CACHE, HEAD), bf16),
             V((ROWS, CACHE, HEAD), bf16),
             V((2, 2, TOK, QKV), f32),
+            V((2, TOK, HEAD), f32),
             V((4, 8, TOK, HEAD), bf16),
             V((2, 2, STRETCH, HEAD), bf16),
-            V((TOK, 1024), bf16),
+            V((4, 4, 2 * TOK, HEAD), f32),
+            V((4, 4, 2 * TOK, HEAD), f32),
+            V((4, 4, 2 * TOK, HEAD), f32),
+            V((4, TOK, 1024), bf16),
             V((4, 4, TOK, PIECE), bf16),
             V((2, 2, TOK, PIECE), bf16),
             V((2, 4, TOK, PIECE), bf16),
             V((STRETCH, HEAD), f32),
             V((STRETCH, HEAD), f32),
-            V((TOK, D), bf16),
             V((8, STRETCH), f32),
+            V((4, TOK, PIECE), bf16),
             V((STEPS, ROWS, D), bf16),
             V((16, D), f32),
             V((16, D), bf16),
@@ -539,7 +611,7 @@
             V((7, 16, 512), bf16),
             V((8, 16, 512), bf16),
             V((16, D), f32),
-            dma((11,)), dma((4,)),
+            dma((14,)),
             dma((2, 6)), dma((3, 4)),
             dma((5,)), dma((5,)),
             dma((8,)), dma((8,)),
@@ -552,13 +624,36 @@
             dma((7,)), dma((7,)),
         ],
         compiler_params=pltpu.CompilerParams(
-            collective_id=0, has_side_effects=True, vmem_limit_bytes=61 * 2**20
+            collective_id=0, has_side_effects=True, vmem_limit_bytes=59 * 2**20
         ),
         name="layer",
     )(
         prompt_len, assign, slot, cache_len, gain.reshape(1, D), jnp.asarray(fr),
         prompt, dec_tokens, cache_k, cache_v, w_qkv, w_out, jnp.asarray(ct), jnp.asarray(st),
     )
+    return pl.pallas_call(
+        writer,
+        out_shape=(
+            jax.ShapeDtypeStruct((1, TOK, D), bf16),
+            jax.ShapeDtypeStruct((STEPS, ROWS, D), bf16),
+        ),
+        in_specs=[vmem, vmem],
+        out_specs=(any_, any_),
+        scratch_shapes=[V((STEPS, ROWS, D), bf16), dma((2,))],
+        compiler_params=pltpu.CompilerParams(vmem_limit_bytes=8 * 2**20),
+        name="write",
+    )(out, dout)
+
+
+def writer(out_ref, dout_ref, full_ref, dec_ref, stage, sem):
+    copies = [pltpu.make_async_copy(out_ref, full_ref.at[0], sem.at[0])]
+    copies[0].start()
+    for s in range(STEPS):
+        stage[s] = dout_ref[pl.ds(s * ROWS, ROWS), :]
+    copies.append(pltpu.make_async_copy(stage, dec_ref, sem.at[1]))
+    copies[1].start()
+    for cp in copies:
+        cp.wait()
 
 
 def solution(mesh):

time: 98.3 us -> 102 us (1.038)
  Pallas kernels: 91.6 us -> 98.9 us
  local copies, waits for them, and re-layouts: 3.89 us -> 0 us
    pallas_call x1 -> x2, Pallas kernels: 91.6 us -> 98.9 us  [the longest x1 97.9 us: body(): pl.pallas_call(kernel, out_shape=(OUT((TOK, D), bf16), OUT((16, D), bf16)...]
    unnamed x2 -> x0, local copies, waits for them, and re-layouts: 3.89 us -> none
where the time goes in v2:
time: 102 us; the launch traced here: 101 us
  Pallas kernels  98.9 us (97%)
  between operations  2.58 us (3%)
    pallas_call x1, Pallas kernels, body(): pl.pallas_call(kernel, out_shape=(OUT((TOK, D), bf16), OUT((16, D), bf16)...  97.9 us

profile of v2, /device:TPU:1, one launch (start us, length us, event | category | flops | bytes accessed | tf_op | source)
XLA Modules:
  0.0 101.5 jit_solution(15387308783332242205)
XLA Ops:
  2.6 97.9 %layer.1 = (bf16[128,4096]{1,0:T(8,128)(2,1)S(1)}, bf16[16,4096]{1,0:T(8,128)(2,1)S(1)}) custom-call(s32[1,1]{1,0:T(1,128)S(6)} %copy.16.plen_ref, s32[1,1]{1,0:T(1,128)S(6)} %copy.17.assign_ref, s32[1,1]{1,0:T(1,128)S(6)} %copy.18.slot_ref, s32[4]{0:T(128)} %clen_ref.1, f32[1,4096]{1,0:T(1,128)} %bitcast.1, f32[8,128]{1,0:T(8,128)} %constant.6.clone.freq_ref, ...), custom_call_target="tpu_custom_call" | custom-call | tf_op jit(solution)/shard_map/layer/pallas_call | solution.py:564
  100.5 1.0 %write.1 = (bf16[1,128,4096]{2,1,0:T(8,128)(2,1)}, bf16[4,4,4096]{2,1,0:T(4,128)(2,1)}) custom-call(bf16[128,4096]{1,0:T(8,128)(2,1)S(1)} %get-tuple-element.4.out_ref, bf16[16,4096]{1,0:T(8,128)(2,1)S(1)} %get-tuple-element.5.dout_ref), custom_call_target="tpu_custom_call" | custom-call | tf_op jit(solution)/shard_map/write/pallas_call | solution.py:634

commit v3 on v2

--- a/solution.py
+++ b/solution.py
@@ -49,12 +49,13 @@
 
 
 def kernel(
-    plen_ref, assign_ref, slot_ref, clen_ref, gain_ref, freq_ref,
+    plen_in, assign_in, slot_in, clen_in, gain_in, freq_in,
     prompt_ref, dec_ref, ck_ref, cv_ref, wqkv_ref, wout_ref, ct_ref, st_ref,
     out_ref, dout_ref,
-    xs, wq, wo, ck, cv, acc, ssq, qs, kv, so, sm, sl, at, pb, fr, nr, ct, st, bias,
-    xn, dmv, x16, xd, qd, kd, vd, qr, ms, ls, os_, plt, pls, qnew, qn, pks, pk, od, dsb, drb, dfb, o32,
-    lsem, agS, agR, wS, wR, plS, plR, qnS, qnR, pkS, pkR, kvS, kvR, fS, fR, nS, nR, dS, dR, eS, eR,
+    plen_ref, assign_ref, slot_ref, clen_ref, gain_ref, freq_ref,
+    xs, wq, wo, ck, cv, acc, ssq, qs, kv, so, sm, at, pb, fr, nr, ct, st, bias,
+    xn, dmv, x16, xd, jd, qd, kd, vd, qr, ms, ls, os_, plt, pls, qnew, qn, pks, pk, od, dsb, drb, dfb, o32,
+    ring, opened, ssem, lsem, agS, agR, wS, wR, plS, plR, qnS, qnR, pkS, pkR, kvS, kvR, fS, fR, nS, nR, dS, dR, eS, eR,
 ):
     me = lax.axis_index("blk")
     pool = lax.axis_index("pool")
@@ -90,20 +91,38 @@
     ldec, w0, t0, w1, t1, w2, t2, w3, t3, lct, lst, lck, lcv, lwo = local
     lweights = (w0, w1, w2, w3)
     ltokens = (t0, t1, t2, t3)
+    small = [
+        pltpu.make_async_copy(a, b, ssem.at[i])
+        for i, (a, b) in enumerate((
+            (plen_in, plen_ref), (assign_in, assign_ref), (slot_in, slot_ref),
+            (clen_in, clen_ref), (gain_in, gain_ref), (freq_in, freq_ref),
+        ))
+    ]
+    for cp in small:
+        cp.start()
     for cp in local:
         cp.start()
 
     barrier = pltpu.get_barrier_semaphore()
+    gate = me == 0
     for j in range(1, 8):
-        pl.semaphore_signal(barrier, inc=1, device_id=peer(j), device_id_type=MESH)
-    for j in range(8):
-        pl.semaphore_signal(barrier, inc=1, device_id=other(j), device_id_type=MESH)
-
-    plt[...] = jnp.full((8, 128), plen_ref[0, 0], jnp.int32)
-    col = lax.broadcasted_iota(jnp.int32, (8, STRETCH), 1)
-    bias[...] = jnp.where(col < jnp.full((8, STRETCH), plen_ref[0, 0], jnp.int32), 0.0, NEG)
-
-    pl.semaphore_wait(barrier, 15)
+        @pl.when(lax.rem(me + j, 8) != 0)
+        def _(j=j):
+            pl.semaphore_signal(barrier, inc=1, device_id=peer(j), device_id_type=MESH)
+
+    kv[:, :, 2 * HEAD:] = jnp.ones((2, STRETCH, HEAD), bf16)
+
+    @pl.when(me != 0)
+    def _():
+        pl.semaphore_wait(barrier, 7)
+
+    @pl.when(me == 1)
+    def _():
+        pl.semaphore_signal(ring, inc=1, device_id=peer(7), device_id_type=MESH)
+
+    @pl.when(gate)
+    def _():
+        pl.semaphore_wait(ring, 1)
 
     def gather(direction, k):
         if direction == 0:
@@ -128,11 +147,16 @@
     for k in range(5):
         weight(k).start()
 
-    def length(j):
-        return remote(plt, pls.at[batch], plS.at[j], plR.at[batch], other(j))
-
-    for j in range(8):
-        length(j).start()
+    @pl.when(gate)
+    def _():
+        for j in range(8):
+            pl.semaphore_signal(barrier, inc=1, device_id=other(j), device_id_type=MESH)
+
+    for cp in small:
+        cp.wait()
+    plt[...] = jnp.full((8, 128), plen_ref[0, 0], jnp.int32)
+    col = lax.broadcasted_iota(jnp.int32, (8, STRETCH), 1)
+    bias[...] = jnp.where(col < jnp.full((8, STRETCH), plen_ref[0, 0], jnp.int32), 0.0, NEG)
 
     ldec.wait()
     for s in range(STEPS):
@@ -144,6 +168,7 @@
     for q in range(4):
         lweights[q].wait()
         joined = joined + dot(xd[:, q * PIECE:(q + 1) * PIECE], wq[0, pl.ds(q * PIECE, PIECE), :])
+    jd[...] = joined
 
     def scaled(slot, q, a):
         wide = xs[slot, q].astype(f32)
@@ -176,39 +201,40 @@
 
     lax.fori_loop(0, 4, own_first, 0)
 
-    wanted = jnp.full((8, 128), assign_ref[0, 0], jnp.int32)
-    newlen = jnp.zeros((8, 128), jnp.int32)
-    for j in range(8):
-        remote(plt, pls.at[j], plS.at[j], plR.at[j], other(j)).wait_recv()
-    for j in range(8):
-        newlen = newlen + jnp.where(wanted == j, pls[j], 0)
-    row = lax.broadcasted_iota(jnp.int32, (16, 128), 0)
-    row_r = lax.rem(row, ROWS)
-    place = jnp.zeros((16, 128), jnp.int32)
-    for r in range(ROWS):
-        place = jnp.where(row_r == r, jnp.full((16, 128), clen_ref[r], jnp.int32), place)
-    fresh = row_r == jnp.full((16, 128), slot_ref[0, 0], jnp.int32)
-    place = jnp.where(fresh, jnp.broadcast_to(newlen[0:1, :], (16, 128)), place) + row // ROWS
-    angle = place.astype(f32) * freq_ref[0:1, :]
-    lane = lax.broadcasted_iota(jnp.int32, (16, 128), 1)
-    dcos = jnp.cos(angle)
-    dsin = jnp.sin(angle)
-    dsin = jnp.where(lane < HEAD // 2, -dsin, dsin)
-
     def turn(u, cosine, sine):
         return u * cosine + pltpu.roll(u, HEAD // 2, 1) * sine
 
-    for h in range(GROUP):
-        qd[pl.ds(h * 16, 16), :] = turn(joined[:, h * HEAD:(h + 1) * HEAD], dcos, dsin)
-    kd[...] = turn(joined[:, GROUP * HEAD:(GROUP + 1) * HEAD], dcos, dsin).astype(bf16)
-    vd[...] = joined[:, (GROUP + 1) * HEAD:].astype(bf16)
-    slots = jnp.full((16, 128), slot_ref[0, 0], jnp.int32)
-    picked = jnp.zeros((16, 128), f32)
-    for r in range(ROWS):
-        part = qd[pl.ds(r, 16, stride=ROWS), :]
-        qr[r] = part.astype(bf16)
-        picked = picked + jnp.where(slots == r, part, 0.0)
-    qnew[...] = picked.astype(bf16)
+    def decode_queries():
+        wanted = jnp.full((8, 128), assign_ref[0, 0], jnp.int32)
+        newlen = jnp.zeros((8, 128), jnp.int32)
+        for j in range(8):
+            remote(plt, pls.at[j], plS.at[j], plR.at[j], other(j)).wait_recv()
+        for j in range(8):
+            newlen = newlen + jnp.where(wanted == j, pls[j], 0)
+        row = lax.broadcasted_iota(jnp.int32, (16, 128), 0)
+        row_r = lax.rem(row, ROWS)
+        place = jnp.zeros((16, 128), jnp.int32)
+        for r in range(ROWS):
+            place = jnp.where(row_r == r, jnp.full((16, 128), clen_ref[r], jnp.int32), place)
+        fresh = row_r == jnp.full((16, 128), slot_ref[0, 0], jnp.int32)
+        place = jnp.where(fresh, jnp.broadcast_to(newlen[0:1, :], (16, 128)), place) + row // ROWS
+        angle = place.astype(f32) * freq_ref[0:1, :]
+        lane = lax.broadcasted_iota(jnp.int32, (16, 128), 1)
+        dcos = jnp.cos(angle)
+        dsin = jnp.sin(angle)
+        dsin = jnp.where(lane < HEAD // 2, -dsin, dsin)
+
+        for h in range(GROUP):
+            qd[pl.ds(h * 16, 16), :] = turn(jd[:, h * HEAD:(h + 1) * HEAD], dcos, dsin)
+        kd[...] = turn(jd[:, GROUP * HEAD:(GROUP + 1) * HEAD], dcos, dsin).astype(bf16)
+        vd[...] = jd[:, (GROUP + 1) * HEAD:].astype(bf16)
+        slots = jnp.full((16, 128), slot_ref[0, 0], jnp.int32)
+        picked = jnp.zeros((16, 128), f32)
+        for r in range(ROWS):
+            part = qd[pl.ds(r, 16, stride=ROWS), :]
+            qr[r] = part.astype(bf16)
+            picked = picked + jnp.where(slots == r, part, 0.0)
+        qnew[...] = picked.astype(bf16)
 
     def origin(slot):
         if isinstance(slot, int):
@@ -217,11 +243,11 @@
 
     def exchange(slot, h):
         rows = pl.ds(pl.multiple_of((origin(slot) * 2 + c) * TOK, TOK), TOK)
-        return remote(kv.at[h, :, rows], kv.at[1 - h, :, rows], kvS.at[slot, h], kvR.at[slot, 1 - h], near(0, 1))
+        return remote(kv.at[h, rows, pl.ds(0, 2 * HEAD)], kv.at[1 - h, rows, pl.ds(0, 2 * HEAD)], kvS.at[slot, h], kvR.at[slot, 1 - h], near(0, 1))
 
     def exchanged(slot, h):
         rows = pl.ds(pl.multiple_of((origin(slot) * 2 + 1 - c) * TOK, TOK), TOK)
-        return remote(kv.at[h, :, rows], kv.at[h, :, rows], kvS.at[slot, h], kvR.at[slot, h], near(0, 1))
+        return remote(kv.at[h, rows, pl.ds(0, 2 * HEAD)], kv.at[h, rows, pl.ds(0, 2 * HEAD)], kvS.at[slot, h], kvR.at[slot, h], near(0, 1))
 
     def finish(slot, a):
         rows = pl.ds(pl.multiple_of((origin(slot) * 2 + c) * TOK, TOK), TOK)
@@ -229,8 +255,8 @@
         cosine = ct[rows, :] * factor
         sine = st[rows, :] * factor
         for h in range(2):
-            kv[h, 0, rows, :] = turn(acc[a, h, :, GROUP * HEAD:(GROUP + 1) * HEAD], cosine, sine).astype(bf16)
-            kv[h, 1, rows, :] = (acc[a, h, :, (GROUP + 1) * HEAD:] * factor).astype(bf16)
+            kv[h, rows, :HEAD] = turn(acc[a, h, :, GROUP * HEAD:(GROUP + 1) * HEAD], cosine, sine).astype(bf16)
+            kv[h, rows, HEAD:2 * HEAD] = (acc[a, h, :, (GROUP + 1) * HEAD:] * factor).astype(bf16)
         for h in range(2):
             for g in range(GROUP):
                 qs[slot, h * GROUP + g] = turn(acc[a, h, :, g * HEAD:(g + 1) * HEAD], cosine, sine).astype(bf16)
@@ -260,16 +286,22 @@
     def query(j):
         return remote(qnew, qn.at[batch], qnS.at[j], qnR.at[batch], other(j))
 
-    lck.wait()
-    lcv.wait()
-
-    def early_row(r, _):
-        old_row(r)
-        return 0
-
-    lax.fori_loop(0, 2, early_row, 0)
+    @pl.when(gate)
+    def _():
+        pl.semaphore_wait(barrier, 8)
+        for j in range(1, 8):
+            pl.semaphore_signal(opened, inc=1, device_id=peer(j), device_id_type=MESH)
+
+    @pl.when(me != 0)
+    def _():
+        pl.semaphore_wait(opened, 1)
+
+    def length(j):
+        return remote(plt, pls.at[batch], plS.at[j], plR.at[batch], other(j))
+
     for j in range(8):
-        query(j).start()
+        length(j).start()
+
     for k in range(4):
         weight(k).wait_recv()
     lct.wait()
@@ -284,6 +316,8 @@
 
     clear(0)
     clear(1)
+    lck.wait()
+    lcv.wait()
 
     def near_step(t, _):
         q1 = t
@@ -299,9 +333,15 @@
         project(1, q1, 0)
         project(2, q2, 1)
 
-        @pl.when(t < 2)
+        @pl.when(t == 1)
         def _():
-            old_row(t + 2)
+            decode_queries()
+            for j in range(2):
+                old_row(j)
+            for j in range(8):
+                query(j).start()
+            for j in range(2, 4):
+                old_row(j)
 
         return 0
 
@@ -311,51 +351,46 @@
 
     def attend_own(d):
         krows = pl.ds(pl.multiple_of(origin(d) * 256, 256), 256)
-
-        def pair(hp, _):
-            q2 = qs[d, pl.ds(hp * 2, 2)].reshape(2 * TOK, HEAD)
+        qi = lax.rem(lax.broadcasted_iota(jnp.int32, (2 * TOK, 256), 0), TOK) + c * TOK
+        ki = lax.broadcasted_iota(jnp.int32, (2 * TOK, 256), 1)
+        mask = jnp.where(ki <= qi, jnp.broadcast_to(bias[0:1, krows], (2 * TOK, 256)), NEG)
+        for hp in range(4):
+            q2 = qs[d, 2 * hp:2 * hp + 2].reshape(2 * TOK, HEAD)
             h = hp // 2
-            s = dot_t(q2, kv[h, 0, krows, :]) * SCALE2 + bias[0:1, krows]
-            qi = lax.rem(lax.broadcasted_iota(jnp.int32, (2 * TOK, 256), 0), TOK) + c * TOK
-            ki = lax.broadcasted_iota(jnp.int32, (2 * TOK, 256), 1)
-            s = jnp.where(ki <= qi, s, NEG)
+            s = dot_t(q2, kv[h, krows, :HEAD]) * SCALE2 + mask
             top = jnp.max(s, axis=-1, keepdims=True)
             p = jnp.exp2(s - top)
             sm[d, hp] = jnp.broadcast_to(top, (2 * TOK, HEAD))
-            sl[d, hp] = jnp.broadcast_to(jnp.sum(p, axis=-1, keepdims=True), (2 * TOK, HEAD))
-            so[d, hp] = dot(p.astype(bf16), kv[h, 1, krows, :])
-            return 0
-
-        lax.fori_loop(0, 4, pair, 0)
+            so[d, hp] = dot(p.astype(bf16), kv[h, krows, HEAD:])
 
     def attend_more(d, k):
         krows = pl.ds(pl.multiple_of(origin(k) * 256, 256), 256)
 
-        def pair(hp, _):
-            q2 = qs[d, pl.ds(hp * 2, 2)].reshape(2 * TOK, HEAD)
-            h = hp // 2
-            s = dot_t(q2, kv[h, 0, krows, :]) * SCALE2 + bias[0:1, krows]
-            before = sm[d, hp]
-            top = jnp.maximum(before, jnp.broadcast_to(jnp.max(s, axis=-1, keepdims=True), (2 * TOK, HEAD)))
-            p = jnp.exp2(s - jnp.concatenate([top, top], axis=1))
-            fade = jnp.exp2(before - top)
-            sm[d, hp] = top
-            sl[d, hp] = sl[d, hp] * fade + jnp.broadcast_to(jnp.sum(p, axis=-1, keepdims=True), (2 * TOK, HEAD))
-            so[d, hp] = so[d, hp] * fade + dot(p.astype(bf16), kv[h, 1, krows, :])
-            return 0
-
         @pl.when(origin(k) < origin(d))
         def _():
-            lax.fori_loop(0, 4, pair, 0)
+            for hp in range(4):
+                q2 = qs[d, 2 * hp:2 * hp + 2].reshape(2 * TOK, HEAD)
+                h = hp // 2
+                s = dot_t(q2, kv[h, krows, :HEAD]) * SCALE2 + bias[0:1, krows]
+                before = sm[d, hp]
+                top = jnp.maximum(before, jnp.broadcast_to(jnp.max(s, axis=-1, keepdims=True), (2 * TOK, HEAD)))
+                p = jnp.exp2(s - jnp.concatenate([top, top], axis=1))
+                fade = jnp.exp2(before - top)
+                sm[d, hp] = top
+                so[d, hp] = so[d, hp] * jnp.concatenate([fade, fade], axis=1) + dot(p.astype(bf16), kv[h, krows, HEAD:])
 
     def attend_near(d):
         attend_own(d)
-        for i in (1, 2) if not isinstance(d, int) else ():
+
+        def others(i, _):
             attend_more(d, lax.rem(d + i, 3))
+            return 0
+
+        lax.fori_loop(1, 3, others, 0)
 
     def settle(d):
         for hp in range(4):
-            o = (so[d, hp] / sl[d, hp]).astype(bf16)
+            o = (so[d, hp, :, :HEAD] / so[d, hp, :, HEAD:]).astype(bf16)
             at[d, :, hp * 256:hp * 256 + HEAD] = o[:TOK]
             at[d, :, hp * 256 + HEAD:(hp + 1) * 256] = o[TOK:]
 
@@ -404,14 +439,13 @@
         for j in range(8):
             remote(qnew, qn.at[j], qnS.at[j], qnR.at[j], other(j)).wait_recv()
         q = qn[...].reshape(8 * 16, HEAD)
-        s = dot_t(q, kv[0, 0]) * SCALE2 + bias[0:1, :]
+        s = dot_t(q, kv[0, :, :HEAD]) * SCALE2 + bias[0:1, :]
         top = jnp.max(s, axis=-1, keepdims=True)
         p = jnp.exp2(s - top)
-        total = jnp.sum(p, axis=-1, keepdims=True)
-        o = dot(p.astype(bf16), kv[0, 1])
-        pks[:, 0] = o.reshape(8, 16, HEAD)
+        o = dot(p.astype(bf16), kv[0, :, HEAD:])
+        pks[:, 0] = o[:, :HEAD].reshape(8, 16, HEAD)
         pks[:, 1] = jnp.broadcast_to(top, (128, HEAD)).reshape(8, 16, HEAD)
-        pks[:, 2] = jnp.broadcast_to(total, (128, HEAD)).reshape(8, 16, HEAD)
+        pks[:, 2] = o[:, HEAD:].reshape(8, 16, HEAD)
 
     def reply(j):
         return remote(pks.at[j], pk.at[batch], pkS.at[j], pkR.at[batch], other(j))
@@ -425,33 +459,34 @@
 
     attend_more(2, 3)
     settle(2)
-    pieces(2, 2, 3)
+    out_piece(2, 2)
     near_send(0, 2).start()
-    near_send(0, 3).start()
     attend_more(1, 3)
     settle(1)
-    pieces(1, 0, 1)
+    out_piece(1, 0)
     near_send(1, 0).start()
+    out_piece(2, 3)
+    near_send(0, 3).start()
+    out_piece(1, 1)
     near_send(1, 1).start()
     answer()
 
     attend_own(3)
+    for j in range(8):
+        reply(j).start()
 
     def far_keys(k, _):
         attend_more(3, k)
         return 0
 
     lax.fori_loop(0, 3, far_keys, 0)
-    for j in range(8):
-        reply(j).start()
     settle(3)
     pieces(3, 0, 2)
     far_send(0).start()
     far_send(2).start()
     pieces(3, 1, 3)
-    far_send(1).start()
-    far_send(3).start()
-
+    pieces(2, 0, 1)
+    pieces(1, 2, 3)
     for j in range(8):
         remote(pks.at[j], pk.at[j], pkS.at[j], pkR.at[j], other(j)).wait_recv()
     want = jnp.full((16, 128), assign_ref[0, 0], jnp.int32)
@@ -463,6 +498,7 @@
         no = no + jnp.where(hit, pk[j, 0], 0.0)
         nm = nm + jnp.where(hit, pk[j, 1], 0.0)
         nl = nl + jnp.where(hit, pk[j, 2], 0.0)
+    slots = jnp.full((16, 128), slot_ref[0, 0], jnp.int32)
     for r in range(ROWS):
         mine = slots == r
         m2 = jnp.where(mine, nm, NEG)
@@ -483,13 +519,23 @@
     for j in range(1, 8):
         scatter(j).start()
 
-    pieces(2, 0, 1)
-    pieces(1, 2, 3)
+    far_send(1).start()
+    far_send(3).start()
+
     attend_more(0, 3)
     settle(0)
     pieces(0, 0, 2)
     pieces(0, 1, 3)
 
+    def relay(q):
+        far_send(q).wait_recv()
+        pb[2, q] = (pb[2, q].astype(f32) + fr[0, q].astype(f32)).astype(bf16)
+        far_send(q + 2).wait_recv()
+        pb[1, q + 2] = (pb[1, q + 2].astype(f32) + fr[1, q].astype(f32)).astype(bf16)
+        near_send(0, q).start()
+        near_send(1, q + 2).start()
+
+    relay(0)
     for j in range(1, 8):
         scatter(j).wait_recv()
     mycols = pl.ds(pl.multiple_of(me * 512, 512), 512)
@@ -506,22 +552,13 @@
     for j in range(1, 8):
         spread(j).start()
 
-    def relay(q):
-        far_send(q).wait_recv()
-        pb[2, q] = (pb[2, q].astype(f32) + fr[0, q].astype(f32)).astype(bf16)
-        far_send(q + 2).wait_recv()
-        pb[1, q + 2] = (pb[1, q + 2].astype(f32) + fr[1, q].astype(f32)).astype(bf16)
-        near_send(0, q).start()
-        near_send(1, q + 2).start()
-
-    relay(0)
+    relay(1)
     for j in range(1, 8):
         spread(j).wait_recv()
     for j in range(1, 8):
         cols = pl.ds(pl.multiple_of(lax.rem(me - j + 8, 8) * 512, 512), 512)
         o32[:, cols] = dfb[j].astype(f32)
     dout_ref[...] = o32[...].astype(bf16)
-    relay(1)
 
     for i, q in enumerate((0, 2, 1, 3)):
         near_send(0, q).wait_recv()
@@ -556,7 +593,6 @@
 ):
     ct, st, fr = tables()
     any_ = pl.BlockSpec(memory_space=pl.ANY)
-    smem = pl.BlockSpec(memory_space=pltpu.SMEM)
     vmem = pl.BlockSpec(memory_space=pltpu.VMEM)
     V = pltpu.VMEM
     dma = pltpu.SemaphoreType.DMA
@@ -567,9 +603,15 @@
             OUT((TOK, D), bf16),
             OUT((16, D), bf16),
         ),
-        in_specs=[smem] * 4 + [vmem] * 2 + [any_] * 8,
+        in_specs=[any_] * 14,
         out_specs=(vmem, vmem),
         scratch_shapes=[
+            pltpu.SMEM((1, 1), jnp.int32),
+            pltpu.SMEM((1, 1), jnp.int32),
+            pltpu.SMEM((1, 1), jnp.int32),
+            pltpu.SMEM((ROWS,), jnp.int32),
+            V((1, D), f32),
+            V((8, HEAD), f32),
             V((4, 4, TOK, PIECE), bf16),
             V((2, D, QKV), bf16),
             V((2, 512, D), bf16),
@@ -578,9 +620,8 @@
             V((2, 2, TOK, QKV), f32),
             V((2, TOK, HEAD), f32),
             V((4, 8, TOK, HEAD), bf16),
-            V((2, 2, STRETCH, HEAD), bf16),
-            V((4, 4, 2 * TOK, HEAD), f32),
-            V((4, 4, 2 * TOK, HEAD), f32),
+            V((2, STRETCH, 3 * HEAD), bf16),
+            V((4, 4, 2 * TOK, 2 * HEAD), f32),
             V((4, 4, 2 * TOK, HEAD), f32),
             V((4, TOK, 1024), bf16),
             V((4, 4, TOK, PIECE), bf16),
@@ -593,6 +634,7 @@
             V((STEPS, ROWS, D), bf16),
             V((16, D), f32),
             V((16, D), bf16),
+            V((16, QKV), f32),
             V((64, HEAD), f32),
             V((16, HEAD), bf16),
             V((16, HEAD), bf16),
@@ -611,6 +653,9 @@
             V((7, 16, 512), bf16),
             V((8, 16, 512), bf16),
             V((16, D), f32),
+            pltpu.SemaphoreType.REGULAR,
+            pltpu.SemaphoreType.REGULAR,
+            dma((6,)),
             dma((14,)),
             dma((2, 6)), dma((3, 4)),
             dma((5,)), dma((5,)),

time: 102 us -> 87.6 us (0.86)
  Pallas kernels: 98.9 us -> 84.7 us
    pallas_call x1, Pallas kernels: 97.9 us -> 83.7 us  [body(): pl.pallas_call(kernel, out_shape=(OUT((TOK, D), bf16), OUT((16, D), bf16)...]
where the time goes in v3:
time: 87.6 us; the launch traced here: 87.4 us
  Pallas kernels  84.7 us (97%)
  between operations  2.74 us (3%)
    pallas_call x1, Pallas kernels, body(): pl.pallas_call(kernel, out_shape=(OUT((TOK, D), bf16), OUT((16, D), bf16)...  83.7 us

profile of v3, /device:TPU:1, one launch (start us, length us, event | category | flops | bytes accessed | tf_op | source)
XLA Modules:
  0.0 87.4 jit_solution(12682256182845511375)
XLA Ops:
  2.6 83.7 %layer.1 = (bf16[128,4096]{1,0:T(8,128)(2,1)S(1)}, bf16[16,4096]{1,0:T(8,128)(2,1)S(1)}) custom-call(s32[1,1]{1,0:T(1,128)S(6)} %copy.16.plen_in, s32[1,1]{1,0:T(1,128)S(6)} %copy.17.assign_in, s32[1,1]{1,0:T(1,128)S(6)} %copy.18.slot_in, s32[4]{0:T(128)} %clen_in.1, f32[1,4096]{1,0:T(1,128)} %bitcast.1, f32[8,128]{1,0:T(8,128)} %constant.6.clone.freq_in, ...), custom_call_target="tpu_custom_call" | custom-call | tf_op jit(solution)/shard_map/layer/pallas_call | solution.py:600
  86.2 1.0 %write.1 = (bf16[1,128,4096]{2,1,0:T(8,128)(2,1)}, bf16[4,4,4096]{2,1,0:T(4,128)(2,1)}) custom-call(bf16[128,4096]{1,0:T(8,128)(2,1)S(1)} %get-tuple-element.4.out_ref, bf16[16,4096]{1,0:T(8,128)(2,1)S(1)} %get-tuple-element.5.dout_ref), custom_call_target="tpu_custom_call" | custom-call | tf_op jit(solution)/shard_map/write/pallas_call | solution.py:679

commit v4 on v3

--- a/solution.py
+++ b/solution.py
@@ -54,8 +54,8 @@
     out_ref, dout_ref,
     plen_ref, assign_ref, slot_ref, clen_ref, gain_ref, freq_ref,
     xs, wq, wo, ck, cv, acc, ssq, qs, kv, so, sm, at, pb, fr, nr, ct, st, bias,
-    xn, dmv, x16, xd, jd, qd, kd, vd, qr, ms, ls, os_, plt, pls, qnew, qn, pks, pk, od, dsb, drb, dfb, o32,
-    ring, opened, ssem, lsem, agS, agR, wS, wR, plS, plR, qnS, qnR, pkS, pkR, kvS, kvR, fS, fR, nS, nR, dS, dR, eS, eR,
+    xn, dmv, x16, xd, jd, qd, kd, vd, qr, ms, ls, os_, plt, pls, qnew, qn, pks, pk, od, hs, hr, dsb, drb, dfb, o32,
+    ring, opened, ssem, lsem, agS, agR, farR, wS, wR, plS, plR, qnS, qnR, pkS, pkR, kvS, kvR, fS, fR, nS, nR, dS, dR,
 ):
     me = lax.axis_index("blk")
     pool = lax.axis_index("pool")
@@ -77,20 +77,24 @@
             src_ref=src, dst_ref=dst, send_sem=ss, recv_sem=rs, device_id=dev, device_id_type=MESH
         )
 
-    local = [pltpu.make_async_copy(dec_ref, dmv, lsem.at[1])]
-    for q in range(4):
-        rows = pl.ds(q * PIECE, PIECE)
-        local.append(pltpu.make_async_copy(wqkv_ref.at[rows], wq.at[0, rows], lsem.at[2 + q]))
-    local.append(pltpu.make_async_copy(ct_ref, ct, lsem.at[6]))
-    local.append(pltpu.make_async_copy(st_ref, st, lsem.at[7]))
-    local.append(pltpu.make_async_copy(ck_ref, ck, lsem.at[8]))
-    local.append(pltpu.make_async_copy(cv_ref, cv, lsem.at[9]))
-    local.append(pltpu.make_async_copy(wout_ref, wo.at[0], lsem.at[10]))
-    for q in range(4):
-        local.insert(2 + 2 * q, pltpu.make_async_copy(prompt_ref.at[0, :, pl.ds(q * PIECE, PIECE)], xs.at[0, q], lsem.at[(0, 11, 12, 13)[q]]))
-    ldec, w0, t0, w1, t1, w2, t2, w3, t3, lct, lst, lck, lcv, lwo = local
-    lweights = (w0, w1, w2, w3)
-    ltokens = (t0, t1, t2, t3)
+    def arrived(ref, sem):
+        remote(ref, ref, sem, sem, near(0, 1)).wait_recv()
+
+    def gone(ref, sem):
+        remote(ref, ref, sem, sem, near(0, 1)).wait_send()
+
+    ldec = pltpu.make_async_copy(dec_ref, dmv, lsem.at[0])
+    lweights = pltpu.make_async_copy(wqkv_ref, wq.at[0], lsem.at[1])
+    ltokens = [
+        pltpu.make_async_copy(prompt_ref.at[0, :, pl.ds(q * PIECE, PIECE)], xs.at[0, q], lsem.at[2])
+        for q in range(4)
+    ]
+    lct = pltpu.make_async_copy(ct_ref, ct, lsem.at[3])
+    lst = pltpu.make_async_copy(st_ref, st, lsem.at[4])
+    lck = pltpu.make_async_copy(ck_ref, ck, lsem.at[5])
+    lcv = pltpu.make_async_copy(cv_ref, cv, lsem.at[6])
+    lwo = pltpu.make_async_copy(wout_ref, wo.at[0], lsem.at[7])
+    local = [ldec, lweights, *ltokens, lct, lst, lck, lcv, lwo]
     small = [
         pltpu.make_async_copy(a, b, ssem.at[i])
         for i, (a, b) in enumerate((
@@ -125,27 +129,26 @@
         pl.semaphore_wait(ring, 1)
 
     def gather(direction, k):
-        if direction == 0:
-            if k < 4:
-                return remote(prompt_ref.at[0, :, pl.ds(k * PIECE, PIECE)], xs.at[1, k], agS.at[0, k], agR.at[0, k], near(1, 0))
-            return remote(xs.at[1, k - 4], xs.at[3, k - 4], agS.at[0, k], agR.at[2, k - 4], near(1, 0))
-        if k < 4:
-            q = (k + 2) % 4
-            return remote(prompt_ref.at[0, :, pl.ds(q * PIECE, PIECE)], xs.at[2, q], agS.at[1, k], agR.at[1, q], near(-1, 0))
-        return remote(xs.at[2, k - 2], xs.at[3, k - 2], agS.at[1, k], agR.at[2, k - 2], near(-1, 0))
+        q = (k + 2 * direction) % 4
+        cols = pl.ds(q * PIECE, PIECE)
+        return remote(
+            prompt_ref.at[0, :, cols], xs.at[1 + direction, q], agS, agR.at[direction, q], near(1 - 2 * direction, 0)
+        )
+
+    def onward(direction, k):
+        q = 2 * direction + (k > 0)
+        cols = pl.ds(0, PIECE) if k == 0 else pl.ds((k - 1) * (PIECE // 2), PIECE // 2)
+        return remote(
+            xs.at[1 + direction, q, :, cols], xs.at[3, q, :, cols], agS, farR.at[direction, k],
+            near(1 - 2 * direction, 0),
+        )
 
     for k in range(4):
         gather(0, k).start()
         gather(1, k).start()
 
-    def weight(k):
-        if k < 4:
-            rows = pl.ds(k * PIECE, PIECE)
-            return remote(wqkv_ref.at[rows], wq.at[1, rows], wS.at[k], wR.at[k], near(0, 1))
-        return remote(wout_ref, wo.at[1], wS.at[4], wR.at[4], near(0, 1))
-
-    for k in range(5):
-        weight(k).start()
+    remote(wqkv_ref, wq.at[1], wS.at[0], wR.at[0], near(0, 1)).start()
+    remote(wout_ref, wo.at[1], wS.at[1], wR.at[1], near(0, 1)).start()
 
     @pl.when(gate)
     def _():
@@ -165,23 +168,23 @@
     factor = lax.rsqrt(jnp.mean(wide * wide, axis=-1, keepdims=True) + EPSILON)
     xd[...] = (wide * factor * gain_ref[...]).astype(bf16)
     joined = jnp.zeros((16, QKV), f32)
+    lweights.wait()
     for q in range(4):
-        lweights[q].wait()
         joined = joined + dot(xd[:, q * PIECE:(q + 1) * PIECE], wq[0, pl.ds(q * PIECE, PIECE), :])
     jd[...] = joined
 
-    def scaled(slot, q, a):
-        wide = xs[slot, q].astype(f32)
+    def scaled(slot, q, a, at=0, size=PIECE):
+        wide = xs[slot, q, :, pl.ds(at, size)].astype(f32)
         square = wide * wide
         part = square[:, :HEAD]
-        for i in range(1, PIECE // HEAD):
+        for i in range(1, size // HEAD):
             part = part + square[:, i * HEAD:(i + 1) * HEAD]
         ssq[a] += part
-        return (wide * gain_ref[:, pl.ds(pl.multiple_of(q * PIECE, PIECE), PIECE)]).astype(bf16)
-
-    def project(slot, q, a):
-        tokens = scaled(slot, q, a)
-        rows = pl.ds(pl.multiple_of(q * PIECE, PIECE), PIECE)
+        return (wide * gain_ref[:, pl.ds(pl.multiple_of(q * PIECE + at, size), size)]).astype(bf16)
+
+    def project(slot, q, a, at=0, size=PIECE):
+        tokens = scaled(slot, q, a, at, size)
+        rows = pl.ds(pl.multiple_of(q * PIECE + at, size), size)
         for h in range(2):
             acc[a, h] += dot(tokens, wq[h, rows, :])
 
@@ -190,8 +193,7 @@
         ssq[a] = jnp.zeros((TOK, HEAD), f32)
 
     clear(0)
-    for q in range(4):
-        ltokens[q].wait()
+    pltpu.make_async_copy(xs.at[0], xs.at[0], lsem.at[2]).wait()
 
     def own_first(q, _):
         tokens = scaled(0, q, 0)
@@ -207,8 +209,7 @@
     def decode_queries():
         wanted = jnp.full((8, 128), assign_ref[0, 0], jnp.int32)
         newlen = jnp.zeros((8, 128), jnp.int32)
-        for j in range(8):
-            remote(plt, pls.at[j], plS.at[j], plR.at[j], other(j)).wait_recv()
+        arrived(pls, plR)
         for j in range(8):
             newlen = newlen + jnp.where(wanted == j, pls[j], 0)
         row = lax.broadcasted_iota(jnp.int32, (16, 128), 0)
@@ -243,11 +244,8 @@
 
     def exchange(slot, h):
         rows = pl.ds(pl.multiple_of((origin(slot) * 2 + c) * TOK, TOK), TOK)
-        return remote(kv.at[h, rows, pl.ds(0, 2 * HEAD)], kv.at[1 - h, rows, pl.ds(0, 2 * HEAD)], kvS.at[slot, h], kvR.at[slot, 1 - h], near(0, 1))
-
-    def exchanged(slot, h):
-        rows = pl.ds(pl.multiple_of((origin(slot) * 2 + 1 - c) * TOK, TOK), TOK)
-        return remote(kv.at[h, rows, pl.ds(0, 2 * HEAD)], kv.at[h, rows, pl.ds(0, 2 * HEAD)], kvS.at[slot, h], kvR.at[slot, h], near(0, 1))
+        cols = pl.ds(0, 2 * HEAD)
+        return remote(kv.at[h, rows, cols], kv.at[1 - h, rows, cols], kvS, kvR.at[slot // 3], near(0, 1))
 
     def finish(slot, a):
         rows = pl.ds(pl.multiple_of((origin(slot) * 2 + c) * TOK, TOK), TOK)
@@ -260,7 +258,6 @@
         for h in range(2):
             for g in range(GROUP):
                 qs[slot, h * GROUP + g] = turn(acc[a, h, :, g * HEAD:(g + 1) * HEAD], cosine, sine).astype(bf16)
-        for h in range(2):
             exchange(slot, h).start()
 
     def old_row(r):
@@ -284,7 +281,7 @@
         os_[r] = mixed
 
     def query(j):
-        return remote(qnew, qn.at[batch], qnS.at[j], qnR.at[batch], other(j))
+        return remote(qnew, qn.at[batch], qnS, qnR, other(j))
 
     @pl.when(gate)
     def _():
@@ -297,13 +294,12 @@
         pl.semaphore_wait(opened, 1)
 
     def length(j):
-        return remote(plt, pls.at[batch], plS.at[j], plR.at[batch], other(j))
+        return remote(plt, pls.at[batch], plS, plR, other(j))
 
     for j in range(8):
         length(j).start()
 
-    for k in range(4):
-        weight(k).wait_recv()
+    arrived(wq.at[1], wR.at[0])
     lct.wait()
     lst.wait()
 
@@ -322,13 +318,19 @@
     def near_step(t, _):
         q1 = t
         q2 = lax.rem(t + 2, 4)
-        remote(xs.at[1, q1], xs.at[1, q1], agS.at[0, q1], agR.at[0, q1], near(1, 0)).wait_recv()
-        remote(xs.at[2, q2], xs.at[2, q2], agS.at[1, q2], agR.at[1, q2], near(1, 0)).wait_recv()
-
-        @pl.when(t < 2)
+        arrived(xs.at[1, q1], agR.at[0, q1])
+        arrived(xs.at[2, q2], agR.at[1, q2])
+
+        @pl.when(t == 0)
         def _():
-            remote(xs.at[1, q1], xs.at[3, q1], agS.at[0, 4 + t], agR.at[2, q1], near(1, 0)).start()
-            remote(xs.at[2, q2], xs.at[3, q2], agS.at[1, 4 + t], agR.at[2, q2], near(-1, 0)).start()
+            onward(0, 0).start()
+            onward(1, 0).start()
+
+        @pl.when(t == 1)
+        def _():
+            for k in (1, 2):
+                onward(0, k).start()
+                onward(1, k).start()
 
         project(1, q1, 0)
         project(2, q2, 1)
@@ -394,9 +396,7 @@
             at[d, :, hp * 256:hp * 256 + HEAD] = o[:TOK]
             at[d, :, hp * 256 + HEAD:(hp + 1) * 256] = o[TOK:]
 
-    for slot in range(3):
-        for h in range(2):
-            exchanged(slot, h).wait_recv()
+    arrived(kv.at[0, pl.ds(0, 6 * TOK), pl.ds(0, 2 * HEAD)], kvR.at[0])
 
     def before_far(i, _):
         attend_near(lax.rem(i + 1, 3))
@@ -406,18 +406,19 @@
 
     clear(0)
 
-    def far_step(t, _):
-        for q in (t, t + 2):
-            remote(xs.at[3, q], xs.at[3, q], agS.at[0, q], agR.at[2, q], near(1, 0)).wait_recv()
-            project(3, q, 0)
-        return 0
-
-    lax.fori_loop(0, 2, far_step, 0)
+    for direction in range(2):
+        arrived(xs.at[3, 2 * direction], farR.at[direction, 0])
+        project(3, 2 * direction, 0)
+    for k in range(2):
+        for direction in range(2):
+            q = 2 * direction + 1
+            half = PIECE // 2
+            arrived(xs.at[3, q, :, pl.ds(k * half, half)], farR.at[direction, 1 + k])
+            project(3, q, 0, k * half, half)
     finish(3, 0)
     lwo.wait()
-    weight(4).wait_recv()
-    for h in range(2):
-        exchanged(3, h).wait_recv()
+    arrived(wo.at[1], wR.at[1])
+    arrived(kv.at[0, pl.ds(0, 2 * TOK), pl.ds(0, 2 * HEAD)], kvR.at[1])
 
     def out_piece(d, q):
         cols = pl.ds(pl.multiple_of(q * PIECE, PIECE), PIECE)
@@ -426,18 +427,17 @@
 
     def far_send(q):
         if q < 2:
-            return remote(pb.at[3, q], fr.at[0, q], fS.at[0, q], fR.at[0, q], near(1, 0))
-        return remote(pb.at[3, q], fr.at[1, q - 2], fS.at[1, q - 2], fR.at[1, q - 2], near(-1, 0))
+            return remote(pb.at[3, q], fr.at[0, q], fS, fR.at[0, q], near(1, 0))
+        return remote(pb.at[3, q], fr.at[1, q - 2], fS, fR.at[1, q - 2], near(-1, 0))
 
     def near_send(direction, q):
         return remote(
-            pb.at[2 - direction, q], nr.at[direction, q], nS.at[direction, q], nR.at[direction, q],
+            pb.at[2 - direction, q], nr.at[direction, q], nS, nR.at[direction, q],
             near(1 - 2 * direction, 0),
         )
 
     def answer():
-        for j in range(8):
-            remote(qnew, qn.at[j], qnS.at[j], qnR.at[j], other(j)).wait_recv()
+        arrived(qn, qnR)
         q = qn[...].reshape(8 * 16, HEAD)
         s = dot_t(q, kv[0, :, :HEAD]) * SCALE2 + bias[0:1, :]
         top = jnp.max(s, axis=-1, keepdims=True)
@@ -448,7 +448,7 @@
         pks[:, 2] = o[:, HEAD:].reshape(8, 16, HEAD)
 
     def reply(j):
-        return remote(pks.at[j], pk.at[batch], pkS.at[j], pkR.at[batch], other(j))
+        return remote(pks.at[j], pk.at[batch], pkS, pkR, other(j))
 
     def pieces(d, first, second):
         def piece(k, _):
@@ -487,8 +487,7 @@
     pieces(3, 1, 3)
     pieces(2, 0, 1)
     pieces(1, 2, 3)
-    for j in range(8):
-        remote(pks.at[j], pk.at[j], pkS.at[j], pkR.at[j], other(j)).wait_recv()
+    arrived(pk, pkR)
     want = jnp.full((16, 128), assign_ref[0, 0], jnp.int32)
     no = jnp.zeros((16, 128), f32)
     nm = jnp.zeros((16, 128), f32)
@@ -510,82 +509,75 @@
     part = jnp.zeros((16, D), f32)
     for h in range(GROUP):
         part = part + dot(od[pl.ds(h * 16, 16), :].astype(bf16), wo[0, pl.ds(h * HEAD, HEAD), :])
-    for k in range(8):
-        dsb[k] = part[:, k * 512:(k + 1) * 512].astype(bf16)
-
-    def scatter(j):
-        return remote(dsb.at[lax.rem(me + j, 8)], drb.at[j - 1], dS.at[j - 1], dR.at[j - 1], peer(j))
-
-    for j in range(1, 8):
-        scatter(j).start()
-
+    o32[...] = part
+
+    def half_cols(core):
+        return pl.ds(pl.multiple_of(core * (D // 2), D // 2), D // 2)
+
+    def chip_cols(core, chip):
+        return pl.ds(pl.multiple_of(core * (D // 2) + chip * 512, 512), 512)
+
+    hs[...] = o32[:, half_cols(1 - c)].astype(bf16)
+    attend_more(0, 3)
+    settle(0)
+    remote(hs, hr, dS.at[0], dR.at[0], near(0, 1)).start()
+    pieces(0, 0, 2)
+    arrived(hr, dR.at[0])
+    o32[:, half_cols(c)] = o32[:, half_cols(c)] + hr[...].astype(f32)
+    for k in range(4):
+        dsb[k] = o32[:, chip_cols(c, lax.rem(x + k, 4))].astype(bf16)
+    for k in range(1, 4):
+        remote(dsb.at[k], drb.at[k - 1], dS.at[1], dR.at[1], near(k, 0)).start()
     far_send(1).start()
     far_send(3).start()
 
-    attend_more(0, 3)
-    settle(0)
-    pieces(0, 0, 2)
     pieces(0, 1, 3)
 
     def relay(q):
-        far_send(q).wait_recv()
+        arrived(fr.at[0, q], fR.at[0, q])
         pb[2, q] = (pb[2, q].astype(f32) + fr[0, q].astype(f32)).astype(bf16)
-        far_send(q + 2).wait_recv()
+        arrived(fr.at[1, q], fR.at[1, q])
         pb[1, q + 2] = (pb[1, q + 2].astype(f32) + fr[1, q].astype(f32)).astype(bf16)
         near_send(0, q).start()
         near_send(1, q + 2).start()
 
     relay(0)
-    for j in range(1, 8):
-        scatter(j).wait_recv()
-    mycols = pl.ds(pl.multiple_of(me * 512, 512), 512)
-    total = dsb[me].astype(f32)
-    for j in range(7):
-        total = total + drb[j].astype(f32)
-    done = (x16[:, mycols] + total).astype(bf16)
-    dfb[0] = done
-    o32[:, mycols] = done.astype(f32)
-
-    def spread(j):
-        return remote(dfb.at[0], dfb.at[j], eS.at[j - 1], eR.at[j - 1], peer(j))
-
-    for j in range(1, 8):
-        spread(j).start()
-
+    arrived(drb, dR.at[1])
+    total = o32[:, chip_cols(c, x)]
+    for k in range(3):
+        total = total + drb[k].astype(f32)
+    dfb[0, 0] = (x16[:, chip_cols(c, x)] + total).astype(bf16)
+    for k in range(1, 4):
+        remote(dfb.at[0, 0], dfb.at[0, k], dS.at[2], dR.at[2], near(k, 0)).start()
     relay(1)
-    for j in range(1, 8):
-        spread(j).wait_recv()
-    for j in range(1, 8):
-        cols = pl.ds(pl.multiple_of(lax.rem(me - j + 8, 8) * 512, 512), 512)
-        o32[:, cols] = dfb[j].astype(f32)
+    arrived(dfb.at[0, pl.ds(1, 3)], dR.at[2])
+    remote(dfb.at[0], dfb.at[1], dS.at[3], dR.at[3], near(0, 1)).start()
+    arrived(dfb.at[1], dR.at[3])
+    for core in range(2):
+        for k in range(4):
+            o32[:, chip_cols(lax.rem(c + core, 2), lax.rem(x - k + 4, 4))] = dfb[core, k].astype(f32)
     dout_ref[...] = o32[...].astype(bf16)
 
     for i, q in enumerate((0, 2, 1, 3)):
-        near_send(0, q).wait_recv()
-        near_send(1, q).wait_recv()
+        arrived(nr.at[0, q], nR.at[0, q])
+        arrived(nr.at[1, q], nR.at[1, q])
         cols = slice(q * PIECE, (q + 1) * PIECE)
         total = pb[0, q].astype(f32) + nr[0, q].astype(f32) + nr[1, q].astype(f32)
         out_ref[:, cols] = (xs[0, q].astype(f32) + total).astype(bf16)
 
-    for k in range(6):
-        gather(0, k).wait_send()
-        gather(1, k).wait_send()
-    for k in range(5):
-        weight(k).wait_send()
-    for j in range(8):
-        length(j).wait_send()
-        query(j).wait_send()
-        reply(j).wait_send()
-    for slot in range(4):
-        for h in range(2):
-            exchange(slot, h).wait_send()
-    for q in range(4):
-        far_send(q).wait_send()
-        near_send(0, q).wait_send()
-        near_send(1, q).wait_send()
-    for j in range(1, 8):
-        scatter(j).wait_send()
-        spread(j).wait_send()
+    gone(xs.at[pl.ds(0, 3)], agS)
+    gone(wq.at[0], wS.at[0])
+    gone(wo.at[0], wS.at[1])
+    gone(pls, plS)
+    gone(qn, qnS)
+    gone(pk, pkS)
+    gone(kv.at[0, :, pl.ds(0, 2 * HEAD)], kvS)
+    gone(pb.at[3], fS)
+    gone(pb.at[pl.ds(1, 2)], nS)
+    gone(hr, dS.at[0])
+    gone(drb, dS.at[1])
+    gone(drb, dS.at[2])
+    gone(dfb.at[0], dS.at[3])
 
 
 def body(
@@ -649,24 +641,22 @@
             V((8, 3, 16, HEAD), f32),
             V((8, 3, 16, HEAD), f32),
             V((64, HEAD), f32),
-            V((8, 16, 512), bf16),
-            V((7, 16, 512), bf16),
-            V((8, 16, 512), bf16),
+            V((16, D // 2), bf16),
+            V((16, D // 2), bf16),
+            V((4, 16, 512), bf16),
+            V((3, 16, 512), bf16),
+            V((2, 4, 16, 512), bf16),
             V((16, D), f32),
             pltpu.SemaphoreType.REGULAR,
             pltpu.SemaphoreType.REGULAR,
-            dma((6,)),
-            dma((14,)),
-            dma((2, 6)), dma((3, 4)),
-            dma((5,)), dma((5,)),
-            dma((8,)), dma((8,)),
-            dma((8,)), dma((8,)),
-            dma((8,)), dma((8,)),
-            dma((4, 2)), dma((4, 2)),
-            dma((2, 2)), dma((2, 2)),
-            dma((2, 4)), dma((2, 4)),
-            dma((7,)), dma((7,)),
-            dma((7,)), dma((7,)),
+            dma((6,)), dma((8,)),
+            dma, dma((2, 4)), dma((2, 3)),
+            dma((2,)), dma((2,)),
+            dma, dma, dma, dma, dma, dma,
+            dma, dma((2,)),
+            dma, dma((2, 2)),
+            dma, dma((2, 4)),
+            dma((4,)), dma((4,)),
         ],
         compiler_params=pltpu.CompilerParams(
             collective_id=0, has_side_effects=True, vmem_limit_bytes=59 * 2**20
@@ -684,19 +674,22 @@
         ),
         in_specs=[vmem, vmem],
         out_specs=(any_, any_),
-        scratch_shapes=[V((STEPS, ROWS, D), bf16), dma((2,))],
+        scratch_shapes=[V((STEPS, ROWS, D), bf16), dma((5,))],
         compiler_params=pltpu.CompilerParams(vmem_limit_bytes=8 * 2**20),
         name="write",
     )(out, dout)
 
 
 def writer(out_ref, dout_ref, full_ref, dec_ref, stage, sem):
-    copies = [pltpu.make_async_copy(out_ref, full_ref.at[0], sem.at[0])]
-    copies[0].start()
+    copies = []
+    for q in range(4):
+        rows = pl.ds(q * 32, 32)
+        copies.append(pltpu.make_async_copy(out_ref.at[rows], full_ref.at[0, rows], sem.at[q]))
+        copies[q].start()
     for s in range(STEPS):
         stage[s] = dout_ref[pl.ds(s * ROWS, ROWS), :]
-    copies.append(pltpu.make_async_copy(stage, dec_ref, sem.at[1]))
-    copies[1].start()
+    copies.append(pltpu.make_async_copy(stage, dec_ref, sem.at[4]))
+    copies[4].start()
     for cp in copies:
         cp.wait()
 

time: 87.6 us -> 84.8 us (0.968)
  Pallas kernels: 84.7 us -> 81.9 us
    pallas_call x1, Pallas kernels: 83.7 us -> 80.8 us  [body(): pl.pallas_call(kernel, out_shape=(OUT((TOK, D), bf16), OUT((16, D), bf16)...]
where the time goes in v4:
time: 84.8 us; the launch traced here: 84.6 us
  Pallas kernels  81.9 us (97%)
  between operations  2.74 us (3%)
    pallas_call x1, Pallas kernels, body(): pl.pallas_call(kernel, out_shape=(OUT((TOK, D), bf16), OUT((16, D), bf16)...  80.8 us

profile of v4, /device:TPU:1, one launch (start us, length us, event | category | flops | bytes accessed | tf_op | source)
XLA Modules:
  0.0 84.6 jit_solution(4035880049009683497)
XLA Ops:
  2.6 80.8 %layer.1 = (bf16[128,4096]{1,0:T(8,128)(2,1)S(1)}, bf16[16,4096]{1,0:T(8,128)(2,1)S(1)}) custom-call(s32[1,1]{1,0:T(1,128)S(6)} %copy.16.plen_in, s32[1,1]{1,0:T(1,128)S(6)} %copy.17.assign_in, s32[1,1]{1,0:T(1,128)S(6)} %copy.18.slot_in, s32[4]{0:T(128)} %clen_in.1, f32[1,4096]{1,0:T(1,128)} %bitcast.1, f32[8,128]{1,0:T(8,128)} %constant.6.clone.freq_in, ...), custom_call_target="tpu_custom_call" | custom-call | tf_op jit(solution)/shard_map/layer/pallas_call | solution.py:592
  83.4 1.0 %write.1 = (bf16[1,128,4096]{2,1,0:T(8,128)(2,1)}, bf16[4,4,4096]{2,1,0:T(4,128)(2,1)}) custom-call(bf16[128,4096]{1,0:T(8,128)(2,1)S(1)} %get-tuple-element.4.out_ref, bf16[16,4096]{1,0:T(8,128)(2,1)S(1)} %get-tuple-element.5.dout_ref), custom_call_target="tpu_custom_call" | custom-call | tf_op jit(solution)/shard_map/write/pallas_call | solution.py:669

commit v5 on v4

--- a/solution.py
+++ b/solution.py
@@ -19,6 +19,7 @@
 ROWS = 4
 QKV = (GROUP + 2) * HEAD
 PIECE = 1024
+PARTS = ((0, 1024), (0, 512), (512, 256), (768, 256))
 EPSILON = 1e-05
 THETA = 500000.0
 NEG = -1e30
@@ -94,7 +95,7 @@
     lck = pltpu.make_async_copy(ck_ref, ck, lsem.at[5])
     lcv = pltpu.make_async_copy(cv_ref, cv, lsem.at[6])
     lwo = pltpu.make_async_copy(wout_ref, wo.at[0], lsem.at[7])
-    local = [ldec, lweights, *ltokens, lct, lst, lck, lcv, lwo]
+    local = [*ltokens, ldec, lweights, lct, lst, lck, lcv, lwo]
     small = [
         pltpu.make_async_copy(a, b, ssem.at[i])
         for i, (a, b) in enumerate((
@@ -102,9 +103,11 @@
             (clen_in, clen_ref), (gain_in, gain_ref), (freq_in, freq_ref),
         ))
     ]
+    for cp in local[:4]:
+        cp.start()
     for cp in small:
         cp.start()
-    for cp in local:
+    for cp in local[4:]:
         cp.start()
 
     barrier = pltpu.get_barrier_semaphore()
@@ -131,19 +134,20 @@
     def gather(direction, k):
         q = (k + 2 * direction) % 4
         cols = pl.ds(q * PIECE, PIECE)
-        return remote(
-            prompt_ref.at[0, :, cols], xs.at[1 + direction, q], agS, agR.at[direction, q], near(1 - 2 * direction, 0)
-        )
+        src = prompt_ref.at[0, :, cols] if k == 0 else xs.at[0, q]
+        return remote(src, xs.at[1 + direction, q], agS, agR.at[direction, q], near(1 - 2 * direction, 0))
 
     def onward(direction, k):
         q = 2 * direction + (k > 0)
-        cols = pl.ds(0, PIECE) if k == 0 else pl.ds((k - 1) * (PIECE // 2), PIECE // 2)
+        cols = pl.ds(*PARTS[k])
         return remote(
             xs.at[1 + direction, q, :, cols], xs.at[3, q, :, cols], agS, farR.at[direction, k],
             near(1 - 2 * direction, 0),
         )
 
     for k in range(4):
+        if k == 1:
+            pltpu.make_async_copy(xs.at[0], xs.at[0], lsem.at[2]).wait()
         gather(0, k).start()
         gather(1, k).start()
 
@@ -193,7 +197,6 @@
         ssq[a] = jnp.zeros((TOK, HEAD), f32)
 
     clear(0)
-    pltpu.make_async_copy(xs.at[0], xs.at[0], lsem.at[2]).wait()
 
     def own_first(q, _):
         tokens = scaled(0, q, 0)
@@ -247,18 +250,29 @@
         cols = pl.ds(0, 2 * HEAD)
         return remote(kv.at[h, rows, cols], kv.at[1 - h, rows, cols], kvS, kvR.at[slot // 3], near(0, 1))
 
-    def finish(slot, a):
+    def factors(slot, a):
         rows = pl.ds(pl.multiple_of((origin(slot) * 2 + c) * TOK, TOK), TOK)
         factor = lax.rsqrt(jnp.sum(ssq[a], axis=-1, keepdims=True) * (1.0 / D) + EPSILON)
-        cosine = ct[rows, :] * factor
-        sine = st[rows, :] * factor
+        return rows, factor, ct[rows, :] * factor, st[rows, :] * factor
+
+    def finish_query(slot, a, h, cosine, sine):
+        for g in range(GROUP):
+            qs[slot, h * GROUP + g] = turn(acc[a, h, :, g * HEAD:(g + 1) * HEAD], cosine, sine).astype(bf16)
+
+    def finish_keys(slot, a):
+        rows, factor, cosine, sine = factors(slot, a)
         for h in range(2):
             kv[h, rows, :HEAD] = turn(acc[a, h, :, GROUP * HEAD:(GROUP + 1) * HEAD], cosine, sine).astype(bf16)
             kv[h, rows, HEAD:2 * HEAD] = (acc[a, h, :, (GROUP + 1) * HEAD:] * factor).astype(bf16)
+        exchange(slot, 0).start()
+        qs[slot, 0] = turn(acc[a, 0, :, :HEAD], cosine, sine).astype(bf16)
+        exchange(slot, 1).start()
+
+    def finish(slot, a):
+        finish_keys(slot, a)
+        rows, factor, cosine, sine = factors(slot, a)
         for h in range(2):
-            for g in range(GROUP):
-                qs[slot, h * GROUP + g] = turn(acc[a, h, :, g * HEAD:(g + 1) * HEAD], cosine, sine).astype(bf16)
-            exchange(slot, h).start()
+            finish_query(slot, a, h, cosine, sine)
 
     def old_row(r):
         q16 = qr[r]
@@ -328,7 +342,7 @@
 
         @pl.when(t == 1)
         def _():
-            for k in (1, 2):
+            for k in (1, 2, 3):
                 onward(0, k).start()
                 onward(1, k).start()
 
@@ -370,16 +384,19 @@
 
         @pl.when(origin(k) < origin(d))
         def _():
-            for hp in range(4):
-                q2 = qs[d, 2 * hp:2 * hp + 2].reshape(2 * TOK, HEAD)
-                h = hp // 2
-                s = dot_t(q2, kv[h, krows, :HEAD]) * SCALE2 + bias[0:1, krows]
-                before = sm[d, hp]
-                top = jnp.maximum(before, jnp.broadcast_to(jnp.max(s, axis=-1, keepdims=True), (2 * TOK, HEAD)))
-                p = jnp.exp2(s - jnp.concatenate([top, top], axis=1))
-                fade = jnp.exp2(before - top)
-                sm[d, hp] = top
-                so[d, hp] = so[d, hp] * jnp.concatenate([fade, fade], axis=1) + dot(p.astype(bf16), kv[h, krows, HEAD:])
+            more_keys(d, krows)
+
+    def more_keys(d, krows):
+        for hp in range(4):
+            q2 = qs[d, 2 * hp:2 * hp + 2].reshape(2 * TOK, HEAD)
+            h = hp // 2
+            s = dot_t(q2, kv[h, krows, :HEAD]) * SCALE2 + bias[0:1, krows]
+            before = sm[d, hp]
+            top = jnp.maximum(before, jnp.broadcast_to(jnp.max(s, axis=-1, keepdims=True), (2 * TOK, HEAD)))
+            p = jnp.exp2(s - jnp.concatenate([top, top], axis=1))
+            fade = jnp.exp2(before - top)
+            sm[d, hp] = top
+            so[d, hp] = so[d, hp] * jnp.concatenate([fade, fade], axis=1) + dot(p.astype(bf16), kv[h, krows, HEAD:])
 
     def attend_near(d):
         attend_own(d)
@@ -404,26 +421,22 @@
 
     lax.fori_loop(0, 3, before_far, 0)
 
-    clear(0)
-
-    for direction in range(2):
-        arrived(xs.at[3, 2 * direction], farR.at[direction, 0])
-        project(3, 2 * direction, 0)
-    for k in range(2):
-        for direction in range(2):
-            q = 2 * direction + 1
-            half = PIECE // 2
-            arrived(xs.at[3, q, :, pl.ds(k * half, half)], farR.at[direction, 1 + k])
-            project(3, q, 0, k * half, half)
-    finish(3, 0)
-    lwo.wait()
-    arrived(wo.at[1], wR.at[1])
-    arrived(kv.at[0, pl.ds(0, 2 * TOK), pl.ds(0, 2 * HEAD)], kvR.at[1])
-
     def out_piece(d, q):
         cols = pl.ds(pl.multiple_of(q * PIECE, PIECE), PIECE)
         part = dot(at[d, :, :512], wo[0, :, cols]) + dot(at[d, :, 512:], wo[1, :, cols])
         pb[d, q] = part.astype(bf16)
+
+    def half_piece(d, q, half):
+        cols = pl.ds(pl.multiple_of(q * PIECE + half * 512, 512), 512)
+        part = dot(at[d, :, :512], wo[0, :, cols]) + dot(at[d, :, 512:], wo[1, :, cols])
+        pb[d, q, :, half * 512:(half + 1) * 512] = part.astype(bf16)
+
+    def half_send(direction, q, half):
+        cols = pl.ds(half * 512, 512)
+        return remote(
+            pb.at[2 - direction, q, :, cols], nr.at[direction, q, :, cols], nS, nR.at[direction, q],
+            near(1 - 2 * direction, 0),
+        )
 
     def far_send(q):
         if q < 2:
@@ -435,6 +448,43 @@
             pb.at[2 - direction, q], nr.at[direction, q], nS, nR.at[direction, q],
             near(1 - 2 * direction, 0),
         )
+
+    clear(0)
+
+    for direction in range(2):
+        arrived(xs.at[3, 2 * direction], farR.at[direction, 0])
+        project(3, 2 * direction, 0)
+    lwo.wait()
+    arrived(wo.at[1], wR.at[1])
+    right_needs = origin(3) < origin(2)
+    left_needs = origin(3) < origin(1)
+
+    @pl.when(jnp.logical_not(right_needs))
+    def _():
+        settle(2)
+        out_piece(2, 2)
+
+    @pl.when(jnp.logical_not(left_needs))
+    def _():
+        settle(1)
+        out_piece(1, 0)
+
+    for k in range(1, 4):
+        for direction in range(2):
+            q = 2 * direction + 1
+            arrived(xs.at[3, q, :, pl.ds(*PARTS[k])], farR.at[direction, k])
+            project(3, q, 0, *PARTS[k])
+
+    @pl.when(jnp.logical_not(right_needs))
+    def _():
+        near_send(0, 2).start()
+
+    @pl.when(jnp.logical_not(left_needs))
+    def _():
+        near_send(1, 0).start()
+
+    finish_keys(3, 0)
+    arrived(kv.at[0, pl.ds(0, 2 * TOK), pl.ds(0, 2 * HEAD)], kvR.at[1])
 
     def answer():
         arrived(qn, qnR)
@@ -457,18 +507,36 @@
 
         lax.fori_loop(0, 2, piece, 0)
 
-    attend_more(2, 3)
-    settle(2)
-    out_piece(2, 2)
-    near_send(0, 2).start()
-    attend_more(1, 3)
-    settle(1)
-    out_piece(1, 0)
-    near_send(1, 0).start()
+    far_rows = pl.ds(pl.multiple_of(origin(3) * 256, 256), 256)
+
+    def near_block(i, _):
+        d = jnp.where(c == 0, 2 - i, 1 + i)
+
+        @pl.when(jnp.where(d == 2, origin(2), origin(1)) > origin(3))
+        def _():
+            more_keys(d, far_rows)
+            settle(d)
+            for half in range(2):
+                half_piece(d, jnp.where(d == 2, 2, 0), half)
+
+                @pl.when(d == 2)
+                def _(half=half):
+                    half_send(0, 2, half).start()
+
+                @pl.when(d == 1)
+                def _(half=half):
+                    half_send(1, 0, half).start()
+
+        return 0
+
+    lax.fori_loop(0, 2, near_block, 0)
     out_piece(2, 3)
     near_send(0, 3).start()
     out_piece(1, 1)
     near_send(1, 1).start()
+    rows3, factor3, cosine3, sine3 = factors(3, 0)
+    for h in range(2):
+        finish_query(3, 0, h, cosine3, sine3)
     answer()
 
     attend_own(3)
@@ -650,7 +718,7 @@
             pltpu.SemaphoreType.REGULAR,
             pltpu.SemaphoreType.REGULAR,
             dma((6,)), dma((8,)),
-            dma, dma((2, 4)), dma((2, 3)),
+            dma, dma((2, 4)), dma((2, 4)),
             dma((2,)), dma((2,)),
             dma, dma, dma, dma, dma, dma,
             dma, dma((2,)),

time: 84.8 us -> 82.9 us (0.978)
  Pallas kernels: 81.9 us -> 80.1 us
    pallas_call x1, Pallas kernels: 80.8 us -> 79 us  [body(): pl.pallas_call(kernel, out_shape=(OUT((TOK, D), bf16), OUT((16, D), bf16)...]
where the time goes in v5:
time: 82.9 us; the launch traced here: 82.8 us
  Pallas kernels  80.1 us (97%)
  between operations  2.74 us (3%)
    pallas_call x1, Pallas kernels, body(): pl.pallas_call(kernel, out_shape=(OUT((TOK, D), bf16), OUT((16, D), bf16)...  79 us

profile of v5, /device:TPU:1, one launch (start us, length us, event | category | flops | bytes accessed | tf_op | source)
XLA Modules:
  0.0 82.8 jit_solution(3578107550078496766)
XLA Ops:
  2.6 79.0 %layer.1 = (bf16[128,4096]{1,0:T(8,128)(2,1)S(1)}, bf16[16,4096]{1,0:T(8,128)(2,1)S(1)}) custom-call(s32[1,1]{1,0:T(1,128)S(6)} %copy.16.plen_in, s32[1,1]{1,0:T(1,128)S(6)} %copy.17.assign_in, s32[1,1]{1,0:T(1,128)S(6)} %copy.18.slot_in, s32[4]{0:T(128)} %clen_in.1, f32[1,4096]{1,0:T(1,128)} %bitcast.1, f32[8,128]{1,0:T(8,128)} %constant.6.clone.freq_in, ...), custom_call_target="tpu_custom_call" | custom-call | tf_op jit(solution)/shard_map/layer/pallas_call | solution.py:660
  81.6 1.0 %write.1 = (bf16[1,128,4096]{2,1,0:T(8,128)(2,1)}, bf16[4,4,4096]{2,1,0:T(4,128)(2,1)}) custom-call(bf16[128,4096]{1,0:T(8,128)(2,1)S(1)} %get-tuple-element.4.out_ref, bf16[16,4096]{1,0:T(8,128)(2,1)S(1)} %get-tuple-element.5.dout_ref), custom_call_target="tpu_custom_call" | custom-call | tf_op jit(solution)/shard_map/write/pallas_call | solution.py:737

commit v6 on v5

--- a/solution.py
+++ b/solution.py
@@ -55,8 +55,8 @@
     out_ref, dout_ref,
     plen_ref, assign_ref, slot_ref, clen_ref, gain_ref, freq_ref,
     xs, wq, wo, ck, cv, acc, ssq, qs, kv, so, sm, at, pb, fr, nr, ct, st, bias,
-    xn, dmv, x16, xd, jd, qd, kd, vd, qr, ms, ls, os_, plt, pls, qnew, qn, pks, pk, od, hs, hr, dsb, drb, dfb, o32,
-    ring, opened, ssem, lsem, agS, agR, farR, wS, wR, plS, plR, qnS, qnR, pkS, pkR, kvS, kvR, fS, fR, nS, nR, dS, dR,
+    xn, dmv, x16, xd, jd, qd, kd, vd, qr, ms, ls, os_, plt, pls, qnew, qn, pks, pk, od, hs, hr, dsb, drb, dfb, lr, lhs, lhr, lsb, lrb, lfb, o32,
+    ring, opened, ssem, lsem, agS, agR, farR, wS, wR, plS, plR, qnS, qnR, pkS, pkR, kvS, kvR, fS, fR, nS, nR, dS, dR, eS, eR,
 ):
     me = lax.axis_index("blk")
     pool = lax.axis_index("pool")
@@ -324,6 +324,28 @@
     lax.fori_loop(0, 4, own_second, 0)
     finish(0, 0)
 
+    def half_cols(core):
+        return pl.ds(pl.multiple_of(core * (D // 2), D // 2), D // 2)
+
+    def chip_cols(core, chip):
+        return pl.ds(pl.multiple_of(core * (D // 2) + chip * 512, 512), 512)
+
+    def early_rows():
+        for r in range(ROWS):
+            od[pl.ds(r, 16, stride=ROWS), :] = os_[r] / ls[r]
+        lwo.wait()
+        part = jnp.zeros((16, D), f32)
+        for h in range(GROUP):
+            part = part + dot(od[pl.ds(h * 16, 16), :].astype(bf16), wo[0, pl.ds(h * HEAD, HEAD), :])
+        o32[...] = part
+        hs[...] = o32[:, half_cols(1 - c)].astype(bf16)
+
+    def early_halves():
+        arrived(hr, dR.at[0])
+        o32[:, half_cols(c)] = o32[:, half_cols(c)] + hr[...].astype(f32)
+        for k in range(4):
+            dsb[k] = o32[:, chip_cols(c, lax.rem(x + k, 4))].astype(bf16)
+
     clear(0)
     clear(1)
     lck.wait()
@@ -358,6 +380,14 @@
                 query(j).start()
             for j in range(2, 4):
                 old_row(j)
+
+        @pl.when(t == 2)
+        def _():
+            early_rows()
+
+        @pl.when(t == 3)
+        def _():
+            remote(hs, hr, dS.at[0], dR.at[0], near(0, 1)).start()
 
         return 0
 
@@ -454,7 +484,7 @@
     for direction in range(2):
         arrived(xs.at[3, 2 * direction], farR.at[direction, 0])
         project(3, 2 * direction, 0)
-    lwo.wait()
+    early_halves()
     arrived(wo.at[1], wR.at[1])
     right_needs = origin(3) < origin(2)
     left_needs = origin(3) < origin(1)
@@ -468,6 +498,9 @@
     def _():
         settle(1)
         out_piece(1, 0)
+
+    for k in range(1, 4):
+        remote(dsb.at[k], drb.at[k - 1], dS.at[1], dR.at[1], near(k, 0)).start()
 
     for k in range(1, 4):
         for direction in range(2):
@@ -484,6 +517,13 @@
         near_send(1, 0).start()
 
     finish_keys(3, 0)
+    arrived(drb, dR.at[1])
+    total = o32[:, chip_cols(c, x)]
+    for k in range(3):
+        total = total + drb[k].astype(f32)
+    dfb[0, 0] = (x16[:, chip_cols(c, x)] + total).astype(bf16)
+    for k in range(1, 4):
+        remote(dfb.at[0, 0], dfb.at[0, k], dS.at[2], dR.at[2], near(k, 0)).start()
     arrived(kv.at[0, pl.ds(0, 2 * TOK), pl.ds(0, 2 * HEAD)], kvR.at[1])
 
     def answer():
@@ -566,65 +606,92 @@
         nm = nm + jnp.where(hit, pk[j, 1], 0.0)
         nl = nl + jnp.where(hit, pk[j, 2], 0.0)
     slots = jnp.full((16, 128), slot_ref[0, 0], jnp.int32)
+    mo = jnp.zeros((16, 128), f32)
+    mm = jnp.zeros((16, 128), f32)
+    ml = jnp.zeros((16, 128), f32)
     for r in range(ROWS):
         mine = slots == r
-        m2 = jnp.where(mine, nm, NEG)
-        top = jnp.maximum(ms[r], m2)
-        a = jnp.exp2(ms[r] - top)
-        b = jnp.exp2(m2 - top)
-        o = (os_[r] * a + no * b) / (ls[r] * a + nl * b)
-        od[pl.ds(r, 16, stride=ROWS), :] = o
+        mo = mo + jnp.where(mine, os_[r], 0.0)
+        mm = mm + jnp.where(mine, ms[r], 0.0)
+        ml = ml + jnp.where(mine, ls[r], 0.0)
+    top = jnp.maximum(mm, nm)
+    a = jnp.exp2(mm - top)
+    b = jnp.exp2(nm - top)
+    o = (mo * a + no * b) / (ml * a + nl * b)
+    head = lax.broadcasted_iota(jnp.int32, (16, 128), 0) // STEPS
     part = jnp.zeros((16, D), f32)
     for h in range(GROUP):
-        part = part + dot(od[pl.ds(h * 16, 16), :].astype(bf16), wo[0, pl.ds(h * HEAD, HEAD), :])
-    o32[...] = part
-
-    def half_cols(core):
-        return pl.ds(pl.multiple_of(core * (D // 2), D // 2), D // 2)
-
-    def chip_cols(core, chip):
-        return pl.ds(pl.multiple_of(core * (D // 2) + chip * 512, 512), 512)
-
-    hs[...] = o32[:, half_cols(1 - c)].astype(bf16)
+        part = part + dot(jnp.where(head == h, o, 0.0).astype(bf16), wo[0, pl.ds(h * HEAD, HEAD), :])
+    part = part[:8] + part[8:]
+    part = part + pltpu.roll(part, 4, 0)
+    first = lax.broadcasted_iota(jnp.int32, (8, 256), 0) < STEPS
+    for k in range(8):
+        lr[:, k * 256:(k + 1) * 256] = jnp.where(
+            first, part[:, k * 512:k * 512 + 256], part[:, k * 512 + 256:(k + 1) * 512]
+        )
+
+    def packed_half(core):
+        return pl.ds(pl.multiple_of(core * 1024, 1024), 1024)
+
+    def packed_chip(core, chip):
+        return pl.ds(pl.multiple_of(core * 1024 + chip * 256, 256), 256)
+
+    lhs[...] = lr[:, packed_half(1 - c)].astype(bf16)
     attend_more(0, 3)
     settle(0)
-    remote(hs, hr, dS.at[0], dR.at[0], near(0, 1)).start()
+    remote(lhs, lhr, eS.at[0], eR.at[0], near(0, 1)).start()
     pieces(0, 0, 2)
-    arrived(hr, dR.at[0])
-    o32[:, half_cols(c)] = o32[:, half_cols(c)] + hr[...].astype(f32)
+    arrived(lhr, eR.at[0])
+    lr[:, packed_half(c)] = lr[:, packed_half(c)] + lhr[...].astype(f32)
     for k in range(4):
-        dsb[k] = o32[:, chip_cols(c, lax.rem(x + k, 4))].astype(bf16)
+        lsb[k] = lr[:, packed_chip(c, lax.rem(x + k, 4))].astype(bf16)
     for k in range(1, 4):
-        remote(dsb.at[k], drb.at[k - 1], dS.at[1], dR.at[1], near(k, 0)).start()
+        remote(lsb.at[k], lrb.at[k - 1], eS.at[1], eR.at[1], near(k, 0)).start()
     far_send(1).start()
     far_send(3).start()
 
     pieces(0, 1, 3)
+    arrived(dfb.at[0, pl.ds(1, 3)], dR.at[2])
+    remote(dfb.at[0], dfb.at[1], dS.at[3], dR.at[3], near(0, 1)).start()
 
     def relay(q):
         arrived(fr.at[0, q], fR.at[0, q])
         pb[2, q] = (pb[2, q].astype(f32) + fr[0, q].astype(f32)).astype(bf16)
+        near_send(0, q).start()
         arrived(fr.at[1, q], fR.at[1, q])
         pb[1, q + 2] = (pb[1, q + 2].astype(f32) + fr[1, q].astype(f32)).astype(bf16)
-        near_send(0, q).start()
         near_send(1, q + 2).start()
 
     relay(0)
-    arrived(drb, dR.at[1])
-    total = o32[:, chip_cols(c, x)]
+    arrived(lrb, eR.at[1])
+    total = lr[:, packed_chip(c, x)]
     for k in range(3):
-        total = total + drb[k].astype(f32)
-    dfb[0, 0] = (x16[:, chip_cols(c, x)] + total).astype(bf16)
+        total = total + lrb[k].astype(f32)
+    pick_i = lax.broadcasted_iota(jnp.int32, (16, 16), 0)
+    pick_j = lax.broadcasted_iota(jnp.int32, (16, 16), 1)
+    pick = pick_j == lax.rem(pick_i, STEPS) * ROWS + jnp.full((16, 16), slot_ref[0, 0], jnp.int32)
+    tokens = dot(jnp.where(pick, 1.0, 0.0).astype(bf16), x16[:, chip_cols(c, x)].astype(bf16))[:8]
+    lfb[0, 0] = (jnp.where(first, tokens[:, :256], tokens[:, 256:]) + total).astype(bf16)
     for k in range(1, 4):
-        remote(dfb.at[0, 0], dfb.at[0, k], dS.at[2], dR.at[2], near(k, 0)).start()
+        remote(lfb.at[0, 0], lfb.at[0, k], eS.at[2], eR.at[2], near(k, 0)).start()
     relay(1)
-    arrived(dfb.at[0, pl.ds(1, 3)], dR.at[2])
-    remote(dfb.at[0], dfb.at[1], dS.at[3], dR.at[3], near(0, 1)).start()
+    arrived(lfb.at[0, pl.ds(1, 3)], eR.at[2])
+    remote(lfb.at[0], lfb.at[1], eS.at[3], eR.at[3], near(0, 1)).start()
     arrived(dfb.at[1], dR.at[3])
+    arrived(lfb.at[1], eR.at[3])
     for core in range(2):
         for k in range(4):
             o32[:, chip_cols(lax.rem(c + core, 2), lax.rem(x - k + 4, 4))] = dfb[core, k].astype(f32)
-    dout_ref[...] = o32[...].astype(bf16)
+            lr[:, packed_chip(lax.rem(c + core, 2), lax.rem(x - k + 4, 4))] = lfb[core, k].astype(f32)
+    here = lax.broadcasted_iota(jnp.int32, (ROWS, 256), 0) == jnp.full((ROWS, 256), slot_ref[0, 0], jnp.int32)
+    for s in range(STEPS):
+        for k in range(8):
+            for half in range(2):
+                cols = slice(k * 512 + half * 256, k * 512 + (half + 1) * 256)
+                late = lr[4 * half + s:4 * half + s + 1, k * 256:(k + 1) * 256]
+                dout_ref[s, :, cols] = jnp.where(
+                    here, jnp.broadcast_to(late, (ROWS, 256)), o32[s * ROWS:(s + 1) * ROWS, cols]
+                ).astype(bf16)
 
     for i, q in enumerate((0, 2, 1, 3)):
         arrived(nr.at[0, q], nR.at[0, q])
@@ -646,6 +713,10 @@
     gone(drb, dS.at[1])
     gone(drb, dS.at[2])
     gone(dfb.at[0], dS.at[3])
+    gone(lhr, eS.at[0])
+    gone(lrb, eS.at[1])
+    gone(lrb, eS.at[2])
+    gone(lfb.at[0], eS.at[3])
 
 
 def body(
@@ -661,7 +732,7 @@
         kernel,
         out_shape=(
             OUT((TOK, D), bf16),
-            OUT((16, D), bf16),
+            OUT((STEPS, ROWS, D), bf16),
         ),
         in_specs=[any_] * 14,
         out_specs=(vmem, vmem),
@@ -695,7 +766,7 @@
             V((16, D), f32),
             V((16, D), bf16),
             V((16, QKV), f32),
-            V((64, HEAD), f32),
+            V((72, HEAD), f32),
             V((16, HEAD), bf16),
             V((16, HEAD), bf16),
             V((ROWS, 16, HEAD), bf16),
@@ -708,12 +779,18 @@
             V((8, 16, HEAD), bf16),
             V((8, 3, 16, HEAD), f32),
             V((8, 3, 16, HEAD), f32),
-            V((64, HEAD), f32),
+            V((72, HEAD), f32),
             V((16, D // 2), bf16),
             V((16, D // 2), bf16),
             V((4, 16, 512), bf16),
             V((3, 16, 512), bf16),
             V((2, 4, 16, 512), bf16),
+            V((8, D // 2), f32),
+            V((8, D // 4), bf16),
+            V((8, D // 4), bf16),
+            V((4, 8, 256), bf16),
+            V((3, 8, 256), bf16),
+            V((2, 4, 8, 256), bf16),
             V((16, D), f32),
             pltpu.SemaphoreType.REGULAR,
             pltpu.SemaphoreType.REGULAR,
@@ -724,6 +801,7 @@
             dma, dma((2,)),
             dma, dma((2, 2)),
             dma, dma((2, 4)),
+            dma((4,)), dma((4,)),
             dma((4,)), dma((4,)),
         ],
         compiler_params=pltpu.CompilerParams(
@@ -742,22 +820,19 @@
         ),
         in_specs=[vmem, vmem],
         out_specs=(any_, any_),
-        scratch_shapes=[V((STEPS, ROWS, D), bf16), dma((5,))],
+        scratch_shapes=[dma((2,))],
         compiler_params=pltpu.CompilerParams(vmem_limit_bytes=8 * 2**20),
         name="write",
     )(out, dout)
 
 
-def writer(out_ref, dout_ref, full_ref, dec_ref, stage, sem):
-    copies = []
-    for q in range(4):
-        rows = pl.ds(q * 32, 32)
-        copies.append(pltpu.make_async_copy(out_ref.at[rows], full_ref.at[0, rows], sem.at[q]))
-        copies[q].start()
-    for s in range(STEPS):
-        stage[s] = dout_ref[pl.ds(s * ROWS, ROWS), :]
-    copies.append(pltpu.make_async_copy(stage, dec_ref, sem.at[4]))
-    copies[4].start()
+def writer(out_ref, dout_ref, full_ref, dec_ref, sem):
+    copies = [
+        pltpu.make_async_copy(out_ref, full_ref.at[0], sem.at[0]),
+        pltpu.make_async_copy(dout_ref, dec_ref, sem.at[1]),
+    ]
+    for cp in copies:
+        cp.start()
     for cp in copies:
         cp.wait()
 

time: 82.9 us -> 82.4 us (level)
  no operation moved by 1% of the time
where the time goes in v6:
time: 82.4 us; the launch traced here: 82.2 us
  Pallas kernels  79.5 us (96%)
  between operations  2.74 us (3%)
    pallas_call x1, Pallas kernels, body(): pl.pallas_call(kernel, out_shape=(OUT((TOK, D), bf16), OUT((STEPS, ROWS,...  78.4 us

profile of v6, /device:TPU:1, one launch (start us, length us, event | category | flops | bytes accessed | tf_op | source)
XLA Modules:
  0.0 82.2 jit_solution(12397163179412338883)
XLA Ops:
  2.6 78.4 %layer.1 = (bf16[128,4096]{1,0:T(8,128)(2,1)S(1)}, bf16[4,4,4096]{2,1,0:T(4,128)(2,1)S(1)}) custom-call(s32[1,1]{1,0:T(1,128)S(6)} %copy.16.plen_in, s32[1,1]{1,0:T(1,128)S(6)} %copy.17.assign_in, s32[1,1]{1,0:T(1,128)S(6)} %copy.18.slot_in, s32[4]{0:T(128)} %clen_in.1, f32[1,4096]{1,0:T(1,128)} %bitcast.1, f32[8,128]{1,0:T(8,128)} %constant.6.clone.freq_in, ...), custom_call_target="tpu_custom_call" | custom-call | tf_op jit(solution)/shard_map/layer/pallas_call | solution.py:731
  81.0 1.0 %write.1 = (bf16[1,128,4096]{2,1,0:T(8,128)(2,1)}, bf16[4,4,4096]{2,1,0:T(4,128)(2,1)}) custom-call(bf16[128,4096]{1,0:T(8,128)(2,1)S(1)} %get-tuple-element.4.out_ref, bf16[4,4,4096]{2,1,0:T(4,128)(2,1)S(1)} %get-tuple-element.5.dout_ref), custom_call_target="tpu_custom_call" | custom-call | tf_op jit(solution)/shard_map/write/pallas_call | solution.py:815

commit v7 on v6

--- a/solution.py
+++ b/solution.py
@@ -19,6 +19,7 @@
 ROWS = 4
 QKV = (GROUP + 2) * HEAD
 PIECE = 1024
+FIRST = ((0, 256), (256, 768))
 PARTS = ((0, 1024), (0, 512), (512, 256), (768, 256))
 EPSILON = 1e-05
 THETA = 500000.0
@@ -457,12 +458,13 @@
         pb[d, q] = part.astype(bf16)
 
     def half_piece(d, q, half):
-        cols = pl.ds(pl.multiple_of(q * PIECE + half * 512, 512), 512)
+        at0, size = FIRST[half]
+        cols = pl.ds(pl.multiple_of(q * PIECE + at0, 256), size)
         part = dot(at[d, :, :512], wo[0, :, cols]) + dot(at[d, :, 512:], wo[1, :, cols])
-        pb[d, q, :, half * 512:(half + 1) * 512] = part.astype(bf16)
+        pb[d, q, :, at0:at0 + size] = part.astype(bf16)
 
     def half_send(direction, q, half):
-        cols = pl.ds(half * 512, 512)
+        cols = pl.ds(*FIRST[half])
         return remote(
             pb.at[2 - direction, q, :, cols], nr.at[direction, q, :, cols], nS, nR.at[direction, q],
             near(1 - 2 * direction, 0),

time: 82.4 us -> 82.3 us (level)
  no operation moved by 1% of the time
where the time goes in v7:
time: 82.3 us; the launch traced here: 82.2 us
  Pallas kernels  79.4 us (96%)
  between operations  2.74 us (3%)
    pallas_call x1, Pallas kernels, body(): pl.pallas_call(kernel, out_shape=(OUT((TOK, D), bf16), OUT((STEPS, ROWS,...  78.4 us

profile of v7, /device:TPU:1, one launch (start us, length us, event | category | flops | bytes accessed | tf_op | source)
XLA Modules:
  0.0 82.2 jit_solution(3196725989456114906)
XLA Ops:
  2.6 78.4 %layer.1 = (bf16[128,4096]{1,0:T(8,128)(2,1)S(1)}, bf16[4,4,4096]{2,1,0:T(4,128)(2,1)S(1)}) custom-call(s32[1,1]{1,0:T(1,128)S(6)} %copy.16.plen_in, s32[1,1]{1,0:T(1,128)S(6)} %copy.17.assign_in, s32[1,1]{1,0:T(1,128)S(6)} %copy.18.slot_in, s32[4]{0:T(128)} %clen_in.1, f32[1,4096]{1,0:T(1,128)} %bitcast.1, f32[8,128]{1,0:T(8,128)} %constant.6.clone.freq_in, ...), custom_call_target="tpu_custom_call" | custom-call | tf_op jit(solution)/shard_map/layer/pallas_call | solution.py:733
  81.0 1.0 %write.1 = (bf16[1,128,4096]{2,1,0:T(8,128)(2,1)}, bf16[4,4,4096]{2,1,0:T(4,128)(2,1)}) custom-call(bf16[128,4096]{1,0:T(8,128)(2,1)S(1)} %get-tuple-element.4.out_ref, bf16[4,4,4096]{2,1,0:T(4,128)(2,1)S(1)} %get-tuple-element.5.dout_ref), custom_call_target="tpu_custom_call" | custom-call | tf_op jit(solution)/shard_map/write/pallas_call | solution.py:817
